TPU v7x, 32 devices: a whole 2x2x4 slice. The times are simulated.
32 devices in a mesh: gz: 8 (over z, y), xy: 4 (over x, core).
Axes of the slice: x: 2, y: 2, z: 4, core: 2. Of those that a mesh axis runs over, the one named last changes fastest.
Arguments:
- up_source: bfloat16 [8, 2, 32, 1024], P('gz', None, None, 'xy'), may hold values from -6 to 6
- down_source: bfloat16 [8, 2, 32, 1024], P('gz', None, None, 'xy'), may hold values from -6 to 6
- source_layer: int32 [32], replicated, may hold values from 0 to 7, as said below
- u_factor: bfloat16 [8, 4, 4, 2, 128, 256], P('gz', 'xy'), may hold values from -0.15625 to 0.15625
- v_factor: bfloat16 [8, 4, 4, 2, 128, 256], P('gz', 'xy'), may hold values from -0.25 to 0.25
- block_rank: int32 [8, 4, 4], P('gz', 'xy'), may hold values from 1 to 4
Outputs:
- up_trace: bfloat16 [8, 2, 32, 1024], P('gz', None, None, 'xy')
- down_trace: bfloat16 [8, 2, 32, 1024], P('gz', None, None, 'xy')
Inputs may be any that keep to these rules, and one draw needn't show every extreme that they name: `source_layer`: the index of the layer slab in which source s lies; source 0 lies in slab 0 and source 1 in slab 8 - 1. `block_rank`: block (i, j) of interface l has rank 32 times this number.
All inputs are finite; a program needn't handle non-finite values.
Results may differ from a plain program's by a relative error of at most 0.007.
Values may be sent and summed in bfloat16 or wider, within the bound.
A program may use at most 64 MiB of HBM per device.

v0:
```python
import functools

import jax
import jax.numpy as jnp
from jax import lax
from jax.experimental import pallas as pl
from jax.experimental.pallas import tpu as pltpu
from jax.sharding import PartitionSpec as P

STEPS = 3
MESH = pl.DeviceIdType.MESH


def kernel(
    layers, n, up_hbm, down_hbm, layer_hbm, u_hbm, v_hbm, rank_hbm, up_out, down_out,
    up_ref, down_ref, layer_ref, rank_ref, down_done,
    u_mem, v_mem, up_all, up_send, up_next, up_last, own_down, down_first, part, part_send,
    twin_part, twin_send, last_in, last_send,
    load_sem, up_ssem, up_rsem, next_ssem, next_rsem, last_ssem, last_rsem,
    first_ssem, first_rsem, part_ssem, part_rsem,
    relay_ssem, twin_ssem, twin_rsem, last_part_ssem, last_part_rsem,
):
    layer = lax.axis_index("gz")
    me = lax.axis_index("xy")
    has_above = layer < layers - 1
    has_below = layer > 0
    rows, width = up_send.shape[1:]
    sources = rows // 2
    max_rank = u_mem.shape[2]
    others = [lax.rem(me + k, n) for k in range(n)]
    core = lax.rem(me, 2)
    twin = me + 1 - 2 * core
    like = [lax.rem(me + 2 * k, n) for k in range(n // 2)]
    unlike = [lax.rem(twin + 2 * k, n) for k in range(n // 2)]
    chip = me // 2

    def remote(src, dst, ssem, rsem, to_layer, to_block):
        return pltpu.make_async_remote_copy(
            src_ref=src, dst_ref=dst, send_sem=ssem, recv_sem=rsem,
            device_id={"gz": to_layer, "xy": to_block}, device_id_type=MESH,
        )

    load_u = pltpu.make_async_copy(u_hbm.at[0, 0], u_mem, load_sem.at[0])
    load_v = pltpu.make_async_copy(v_hbm.at[0, 0], v_mem, load_sem.at[1])
    small = [
        pltpu.make_async_copy(src, dst, load_sem.at[2 + i])
        for i, (src, dst) in enumerate(
            [(layer_hbm, layer_ref), (up_hbm.at[0], up_ref), (down_hbm.at[0], down_ref), (rank_hbm, rank_ref)]
        )
    ]
    for load in small:
        load.start()

    barrier = pltpu.get_barrier_semaphore()

    def greet(to_layer, to_block):
        pl.semaphore_signal(
            barrier, inc=1, device_id={"gz": to_layer, "xy": to_block}, device_id_type=MESH
        )

    for k in range(1, n):
        greet(layer, others[k])

    @pl.when(has_above)
    def _():
        for k in range(n // 2):
            greet(layer + 1, like[k])

    @pl.when(has_below)
    def _():
        for k in range(n // 2):
            greet(layer - 1, like[k])

    load_v.start()
    load_u.start()
    for load in small:
        load.wait()
    square = (sources, sources)
    diagonal = lax.broadcasted_iota(jnp.int32, square, 0) == lax.broadcasted_iota(jnp.int32, square, 1)
    source_layer = jnp.sum(
        jnp.where(diagonal, jnp.broadcast_to(layer_ref[...], square), 0), axis=1, keepdims=True
    )
    source_layer = jnp.broadcast_to(jnp.concatenate([source_layer, source_layer], axis=0), (rows, width))
    up_own = jnp.where(
        layer >= source_layer, up_ref[...].reshape(rows, width).astype(jnp.float32), 0.0
    ).astype(jnp.bfloat16)
    down_own = jnp.where(
        layer <= source_layer, down_ref[...].reshape(rows, width).astype(jnp.float32), 0.0
    ).astype(jnp.bfloat16)
    up_all[0, me] = up_own
    own_down[...] = down_own

    @pl.when(jnp.logical_not(has_above))
    def _():
        up_next[...] = jnp.zeros_like(up_next)
        down_first[...] = jnp.zeros_like(down_first)
        part[0] = jnp.zeros_like(part[0])
        part[1] = jnp.zeros_like(part[1])

    peers = n - 1 + jnp.where(has_above, n // 2, 0) + jnp.where(has_below, n // 2, 0)
    pl.semaphore_wait(barrier, peers)

    def gather(k):
        return remote(
            up_all.at[0, me], up_all.at[0, me], up_ssem.at[0, k], up_rsem.at[0, me], layer, others[k]
        )

    def next_up():
        return remote(up_all.at[0, me], up_next, next_ssem, next_rsem, layer - 1, me)

    def first_down():
        return remote(own_down, down_first, first_ssem, first_rsem, layer - 1, me)

    def up_step(t, k):
        return remote(
            up_send.at[t], up_all.at[t + 1, me], up_ssem.at[t + 1, k], up_rsem.at[t + 1, me],
            layer + 1, like[k],
        )

    def relay(t, k):
        slot = up_all.at[t, like[k]]
        return remote(slot, slot, relay_ssem.at[t - 1, k], up_rsem.at[t, like[k]], layer, twin)

    def last_up():
        return remote(up_send.at[STEPS - 1], up_last, last_ssem, last_rsem, layer + 1, me)

    def part_step(t, k):
        return remote(
            part_send.at[t, k], part.at[t, chip], part_ssem.at[t, k], part_rsem.at[t, chip],
            layer - 1, like[k],
        )

    def twin_step(t, k):
        place = unlike[k] // 2
        return remote(
            twin_send.at[t, k], twin_part.at[t, place], twin_ssem.at[t, k], twin_rsem.at[t, place],
            layer, twin,
        )

    def last_part(k):
        return remote(
            last_send.at[k], last_in.at[me], last_part_ssem.at[k], last_part_rsem.at[me],
            layer, others[k],
        )

    def arrived(ref, rsem):
        remote(ref, ref, next_ssem, rsem, layer, me).wait_recv()

    far_first = [*range(2, n), 1]
    for k in far_first:
        gather(k).start()

    @pl.when(has_below)
    def _():
        first_down().start()
        next_up().start()

    rank_index = lax.broadcasted_iota(jnp.int32, (sources, max_rank), 1)

    def coefficients(trace, factor, block):
        product = lax.dot_general(
            trace, factor.reshape(2 * max_rank, width), (((1,), (1,)), ((), ())),
            preferred_element_type=jnp.float32,
        )
        keep = rank_index < (max_rank // 4) * rank_ref[0, 0, block]
        real = product[:sources, :max_rank] - product[sources:, max_rank:]
        imag = product[:sources, max_rank:] + product[sources:, :max_rank]
        real = jnp.where(keep, real, 0.0)
        imag = jnp.where(keep, imag, 0.0)
        return jnp.concatenate(
            [jnp.concatenate([real, -imag], axis=1), jnp.concatenate([imag, real], axis=1)], axis=0
        ).astype(jnp.bfloat16)

    def expand(coef, factor):
        return jnp.dot(
            coef, factor.reshape(2 * max_rank, width), preferred_element_type=jnp.float32
        )

    load_v.wait()
    load_u.wait()

    def wait_blocks(t, blocks):
        for block in blocks:
            arrived(up_all.at[t, block], up_rsem.at[t, block])

    for t in range(STEPS):
        last = t == STEPS - 1
        held = 0 if t == 0 else jnp.where(has_below, t, 0)

        def rise(block):
            return expand(coefficients(up_all[held, block], v_mem[block], block), u_mem[block])

        def piece(block):
            return expand(coefficients(down, u_mem[block], block), v_mem[block])

        if t > 0:

            @pl.when(has_below)
            def _():
                for k in reversed(range(n // 2)):
                    wait_blocks(t, [like[k]])
                    relay(t, k).start()

        @pl.when(has_above)
        def _():
            if t == 0:
                arrived(down_first, first_rsem)
            else:
                for k in range(n // 2):
                    place = like[k] // 2
                    arrived(part.at[t - 1, place], part_rsem.at[t - 1, place])

        down = down_first[...]
        if t > 0:
            total = down.astype(jnp.float32)
            for k in range(n // 2):
                total = total + part[t - 1, like[k] // 2].astype(jnp.float32)
            down = total.astype(jnp.bfloat16)

        if last:
            for k in far_first:
                last_send[k] = piece(others[k]).astype(jnp.bfloat16)
                last_part(k).start()
        else:
            for k in range(n // 2):
                twin_send[t, k] = piece(unlike[k]).astype(jnp.bfloat16)
                twin_step(t, k).start()

        if t == 0:
            wait_blocks(0, like[1:])
        total = sum([rise(block) for block in like])
        if t == 0:
            wait_blocks(0, unlike)

            @pl.when(has_above)
            def _():
                arrived(up_next, next_rsem)

        else:

            @pl.when(has_below)
            def _():
                wait_blocks(t, unlike)

        total = total + sum([rise(block) for block in unlike])
        up_send[t] = (up_next[...].astype(jnp.float32) + total).astype(jnp.bfloat16)

        @pl.when(has_above)
        def _():
            if last:
                last_up().start()
            else:
                for k in reversed(range(n // 2)):
                    up_step(t, k).start()

        if last:
            own_part = piece(me)
        else:
            pieces = [piece(block) for block in like]
            for k in range(n // 2):
                place = like[k] // 2
                arrived(twin_part.at[t, place], twin_rsem.at[t, place])
                part_send[t, k] = (pieces[k] + twin_part[t, place].astype(jnp.float32)).astype(
                    jnp.bfloat16
                )

            @pl.when(has_below)
            def _():
                for k in reversed(range(n // 2)):
                    part_step(t, k).start()

    total = own_down[...].astype(jnp.float32) + own_part
    for k in range(1, n):
        arrived(last_in.at[others[k]], last_part_rsem.at[others[k]])
        total = total + last_in[others[k]].astype(jnp.float32)
    down_done[...] = total.astype(jnp.bfloat16).reshape(2, sources, width)
    put_down = pltpu.make_async_copy(down_done, down_out.at[0], load_sem.at[0])
    put_down.start()

    @pl.when(has_below)
    def _():
        arrived(up_last, last_rsem)
        up_ref[...] = up_last[...].reshape(2, sources, width)

    @pl.when(jnp.logical_not(has_below))
    def _():
        up_ref[...] = up_all[0, me].reshape(2, sources, width)

    put_up = pltpu.make_async_copy(up_ref, up_out.at[0], load_sem.at[1])
    put_up.start()

    for k in range(1, n):
        gather(k).wait_send()
        last_part(k).wait_send()
    for t in range(STEPS - 1):
        for k in range(n // 2):
            twin_step(t, k).wait_send()

    @pl.when(has_below)
    def _():
        first_down().wait_send()
        next_up().wait_send()
        for t in range(STEPS - 1):
            for k in range(n // 2):
                part_step(t, k).wait_send()
                relay(t + 1, k).wait_send()

    @pl.when(has_above)
    def _():
        for t in range(STEPS - 1):
            for k in range(n // 2):
                up_step(t, k).wait_send()
        last_up().wait_send()

    put_down.wait()
    put_up.wait()


def hand_over(up_ref, down_ref, up_out, down_out, up_mem, down_mem, sems):
    pairs = [(up_ref, up_mem, up_out), (down_ref, down_mem, down_out)]
    loads = [pltpu.make_async_copy(src, mem, sems.at[0, i]) for i, (src, mem, _) in enumerate(pairs)]
    stores = [pltpu.make_async_copy(mem, dst, sems.at[1, i]) for i, (_, mem, dst) in enumerate(pairs)]
    for load in loads:
        load.start()
    for load, store in zip(loads, stores):
        load.wait()
        store.start()
    for store in stores:
        store.wait()


def solution(mesh):
    layers, n = mesh.shape["gz"], mesh.shape["xy"]

    def on_device(up_source, down_source, source_layer, u_factor, v_factor, block_rank):
        _, _, sources, width = up_source.shape
        rows = 2 * sources
        trace = (rows, width)
        anywhere = pl.BlockSpec(memory_space=pl.ANY)
        hbm = pl.BlockSpec(memory_space=pltpu.HBM)
        dma = pltpu.SemaphoreType.DMA
        traces = pl.pallas_call(
            functools.partial(kernel, layers, n),
            out_shape=(
                jax.ShapeDtypeStruct(up_source.shape, jnp.bfloat16),
                jax.ShapeDtypeStruct(down_source.shape, jnp.bfloat16),
            ),
            in_specs=[hbm] * 6,
            out_specs=(anywhere, anywhere),
            scratch_shapes=[
                pltpu.VMEM((2, sources, width), jnp.bfloat16),
                pltpu.VMEM((2, sources, width), jnp.bfloat16),
                pltpu.VMEM((1, sources), jnp.int32),
                pltpu.SMEM(block_rank.shape, jnp.int32),
                pltpu.VMEM((2, sources, width), jnp.bfloat16),
                pltpu.VMEM(u_factor.shape[2:], jnp.bfloat16),
                pltpu.VMEM(v_factor.shape[2:], jnp.bfloat16),
                pltpu.VMEM((STEPS, n, *trace), jnp.bfloat16),
                pltpu.VMEM((STEPS, *trace), jnp.bfloat16),
                pltpu.VMEM(trace, jnp.bfloat16),
                pltpu.VMEM(trace, jnp.bfloat16),
                pltpu.VMEM(trace, jnp.bfloat16),
                pltpu.VMEM(trace, jnp.bfloat16),
                pltpu.VMEM((STEPS - 1, n // 2, *trace), jnp.bfloat16),
                pltpu.VMEM((STEPS - 1, n // 2, *trace), jnp.bfloat16),
                pltpu.VMEM((STEPS - 1, n // 2, *trace), jnp.bfloat16),
                pltpu.VMEM((STEPS - 1, n // 2, *trace), jnp.bfloat16),
                pltpu.VMEM((n, *trace), jnp.bfloat16),
                pltpu.VMEM((n, *trace), jnp.bfloat16),
                dma((6,)),
                dma((STEPS, n)),
                dma((STEPS, n)),
                dma,
                dma,
                dma,
                dma,
                dma,
                dma,
                dma((STEPS - 1, n // 2)),
                dma((STEPS - 1, n // 2)),
                dma((STEPS - 1, n // 2)),
                dma((STEPS - 1, n // 2)),
                dma((STEPS - 1, n // 2)),
                dma((n,)),
                dma((n,)),
            ],
            compiler_params=pltpu.CompilerParams(
                collective_id=0, has_side_effects=True
            ),
        )(up_source, down_source, source_layer.reshape(1, sources), u_factor, v_factor, block_rank)
        return pl.pallas_call(
            hand_over,
            out_shape=(
                jax.ShapeDtypeStruct(up_source.shape, jnp.bfloat16),
                jax.ShapeDtypeStruct(down_source.shape, jnp.bfloat16),
            ),
            in_specs=[anywhere, anywhere],
            out_specs=(anywhere, anywhere),
            scratch_shapes=[
                pltpu.VMEM(up_source.shape, jnp.bfloat16),
                pltpu.VMEM(down_source.shape, jnp.bfloat16),
                dma((2, 2)),
            ],
        )(*traces)

    in_specs = (
        P("gz", None, None, "xy"),
        P("gz", None, None, "xy"),
        P(),
        P("gz", "xy", None, None, None, None),
        P("gz", "xy", None, None, None, None),
        P("gz", "xy", None),
    )
    out_specs = (P("gz", None, None, "xy"), P("gz", None, None, "xy"))
    return jax.shard_map(
        on_device, mesh=mesh, in_specs=in_specs, out_specs=out_specs, check_vma=False
    )
```

profile of v0, /device:TPU:8, one launch (start us, length us, event | category | flops | bytes accessed | tf_op | source)
XLA Modules:
  0.0 26.3 jit_solution(17076548757866172997)
XLA Ops:
  0.6 24.3 %shard_map.77 = (bf16[1,2,32,256]{3,2,1,0:T(8,128)(2,1)}, bf16[1,2,32,256]{3,2,1,0:T(8,128)(2,1)}) custom-call(bf16[1,2,32,256]{3,2,1,0:T(8,128)(2,1)} %up_hbm.1, bf16[1,2,32,256]{3,2,1,0:T(8,128)(2,1)} %down_hbm.1, s32[1,32]{1,0:T(1,128)} %bitcast.1, bf16[1,1,4,2,128,256]{5,4,3,2,1,0:T(8,128)(2,1)} %u_hbm.1, bf16[1,1,4,2,128,256]{5,4,3,2,1,0:T(8,128)(2,1)} %v_hbm.1, ...), custom_call_target="tpu_custom_call" | custom-call | tf_op jit(solution)/shard_map/pallas_call | solution.py:342
  24.9 1.4 %shard_map.78 = (bf16[1,2,32,256]{3,2,1,0:T(8,128)(2,1)}, bf16[1,2,32,256]{3,2,1,0:T(8,128)(2,1)}) custom-call(bf16[1,2,32,256]{3,2,1,0:T(8,128)(2,1)} %get-tuple-element.4.up_ref, bf16[1,2,32,256]{3,2,1,0:T(8,128)(2,1)} %get-tuple-element.5.down_ref), custom_call_target="tpu_custom_call" | custom-call | tf_op jit(solution)/shard_map/pallas_call | solution.py:391
where the time goes:
time: 26.6 us; the launch traced here: 26.3 us
  Pallas kernels  25.7 us (97%)
  between operations  0.64 us (2%)
    pallas_call x1, Pallas kernels, on_device(): pl.pallas_call(functools.partial(kernel, layers, n), out_shape=(jax.Shape...  24.3 us
    pallas_call x1, Pallas kernels, on_device(): pl.pallas_call(hand_over, out_shape=(jax.ShapeDtypeStruct(up_source.shape...  1.42 us

commit v1 on v0

v1 whole, which is shorter than its diff:
```python
import functools

import jax
import jax.numpy as jnp
from jax import lax
from jax.experimental import pallas as pl
from jax.experimental.pallas import tpu as pltpu
from jax.sharding import PartitionSpec as P

STEPS = 3
MESH = pl.DeviceIdType.MESH
F32, BF16 = jnp.float32, jnp.bfloat16


def kernel(
    layers, n, up_hbm, down_hbm, layer_hbm, u_hbm, v_hbm, rank_hbm, up_out, down_out,
    up_ref, down_ref, layer_ref, rank_ref, u_mem, v_mem,
    up_own, down_own, up_all, first_in, forward_mem, backward_mem,
    first_term, twin_term, base, up_in, up_send, down_in, down_send,
    up_last_in, up_last_send, down_last_in, down_last_send,
    small_sem, u_sem, v_sem, gather_ssem, gather_rsem, first_ssem, first_rsem,
    back_ssem, back_rsem, forw_ssem, forw_rsem, term_ssem, term_rsem,
    up_ssem0, up_rsem0, up_ssem, up_rsem, up_last_ssem, up_last_rsem,
    down_ssem, down_rsem, down_last_ssem, down_last_rsem,
):
    layer = lax.axis_index("gz")
    me = lax.axis_index("xy")
    has_above = layer < layers - 1
    has_below = layer > 0
    chips = n // 2
    chip = me // 2
    core = lax.rem(me, 2)
    twin = me + 1 - 2 * core
    _, sources, width = up_ref.shape
    half = sources // 2
    rows = 2 * half
    max_rank = u_mem.shape[2]
    chip_order = [lax.rem(chip + k, chips) for k in range(chips)]
    far_chips = [*chip_order[1:], chip]

    def remote(src, dst, ssem, rsem, to_layer, to_block):
        return pltpu.make_async_remote_copy(
            src_ref=src, dst_ref=dst, send_sem=ssem, recv_sem=rsem,
            device_id={"gz": to_layer, "xy": to_block}, device_id_type=MESH,
        )

    def arrived(ref, rsem):
        remote(ref, ref, term_ssem, rsem, layer, me).wait_recv()

    barrier = pltpu.get_barrier_semaphore()

    def greet(to_layer, to_block):
        pl.semaphore_signal(
            barrier, inc=1, device_id={"gz": to_layer, "xy": to_block}, device_id_type=MESH
        )

    @pl.when(has_below)
    def _():
        for k in range(n):
            greet(layer - 1, k)

    @pl.when(has_above)
    def _():
        for k in range(n):
            greet(layer + 1, k)

    for k in range(1, n):
        greet(layer, lax.rem(me + k, n))

    small = [
        pltpu.make_async_copy(src, dst, small_sem.at[i])
        for i, (src, dst) in enumerate(
            [(layer_hbm, layer_ref), (up_hbm.at[0], up_ref), (down_hbm.at[0], down_ref), (rank_hbm, rank_ref)]
        )
    ]
    for load in small:
        load.start()
    load_u = [pltpu.make_async_copy(u_hbm.at[0, 0, j], u_mem.at[j], u_sem.at[j]) for j in range(n)]
    load_v = [pltpu.make_async_copy(v_hbm.at[0, 0, j], v_mem.at[j], v_sem.at[j]) for j in range(n)]
    for j in range(n):
        load_u[j].start()
        load_v[j].start()
    for load in small:
        load.wait()

    square = (sources, sources)
    diagonal = lax.broadcasted_iota(jnp.int32, square, 0) == lax.broadcasted_iota(jnp.int32, square, 1)
    source_layer = jnp.sum(
        jnp.where(diagonal, jnp.broadcast_to(layer_ref[...], square), 0), axis=1, keepdims=True
    )
    source_layer = jnp.broadcast_to(source_layer, (sources, width))
    for ref, own, keep in (
        (up_ref, up_own, layer >= source_layer), (down_ref, down_own, layer <= source_layer),
    ):
        for part in range(2):
            masked = jnp.where(keep, ref[part].astype(F32), 0.0).astype(BF16)
            for h in range(2):
                own[h, part * half:(part + 1) * half] = masked[h * half:(h + 1) * half]

    @pl.when(jnp.logical_not(has_below))
    def _():
        up_in[...] = jnp.zeros_like(up_in)
        up_last_in[...] = jnp.zeros_like(up_last_in)

    @pl.when(jnp.logical_not(has_above))
    def _():
        first_in[...] = jnp.zeros_like(first_in)
        down_in[...] = jnp.zeros_like(down_in)

    peers = n - 1 + jnp.where(has_above, n, 0) + jnp.where(has_below, n, 0)
    pl.semaphore_wait(barrier, peers)

    def gather(k):
        to = lax.rem(me + k, n)
        return remote(up_own, up_all.at[me], gather_ssem.at[k], gather_rsem.at[me], layer, to)

    def first(h):
        return remote(
            down_own.at[h], first_in.at[core], first_ssem.at[h], first_rsem.at[core], layer - 1, 2 * chip + h
        )

    def give_backward(j):
        slot = backward_mem.at[j, core]
        return remote(slot, slot, back_ssem.at[j], back_rsem.at[j], layer, twin)

    def give_forward(j):
        slot = forward_mem.at[core, j]
        return remote(slot, slot, forw_ssem.at[j], forw_rsem.at[j], layer, twin)

    give_term = remote(twin_term, first_term.at[core], term_ssem, term_rsem, layer, twin)

    def up_step0(q, h):
        return remote(
            up_send.at[0, h], up_in.at[0, me], up_ssem0.at[2 * q + h], up_rsem0.at[me], layer + 1, 2 * q + h
        )

    def up_step1(q):
        return remote(
            up_send.at[1], up_in.at[1, pl.ds(2 * chip, 2)], up_ssem.at[q], up_rsem.at[chip],
            layer + 1, 2 * q + core,
        )

    def up_last(h):
        return remote(
            up_last_send.at[h], up_last_in.at[core], up_last_ssem.at[h], up_last_rsem.at[core],
            layer + 1, 2 * chip + h,
        )

    def down_step(t, q):
        return remote(
            down_send.at[t, pl.ds(2 * q, 2)], down_in.at[t, chip], down_ssem.at[t, q], down_rsem.at[t, chip],
            layer - 1, 2 * q + core,
        )

    def down_last(k):
        to = lax.rem(me + k, n)
        return remote(
            down_last_send.at[to], down_last_in.at[me], down_last_ssem.at[k], down_last_rsem.at[me], layer, to
        )

    far_first = [*range(2, n), 1]

    @pl.when(has_below)
    def _():
        for h in range(2):
            first(h).start()

    for k in far_first:
        gather(k).start()

    rank_index = lax.rem(lax.broadcasted_iota(jnp.int32, (2 * max_rank, width), 0), max_rank)

    def factors(j):
        keep = rank_index < (max_rank // 4) * rank_ref[0, 0, j]
        u = u_mem[j].reshape(2 * max_rank, width)
        return jnp.where(keep, u, jnp.zeros_like(u)), v_mem[j].reshape(2 * max_rank, width)

    def paired(x):
        return jnp.concatenate([x[:max_rank], -x[max_rank:]], axis=0), jnp.concatenate(
            [x[max_rank:], x[:max_rank]], axis=0
        )

    def outer(a, b):
        return lax.dot_general(a, b, (((0,), (0,)), ((), ())), preferred_element_type=F32).astype(BF16)

    for j in range(n):
        load_u[j].wait()
        load_v[j].wait()
        u, v = factors(j)
        for part, right in enumerate(paired(v)):
            backward_mem[j, core, part] = outer(u, right)
        give_backward(j).start()
    for j in range(n):
        u, v = factors(j)
        for part, right in enumerate(paired(u)):
            forward_mem[core, j, part] = outer(v, right)
        give_forward(j).start()

    def with_turned(x):
        turned = []
        for k in range(0, x.shape[0], rows):
            turned += [-x[k + half:k + rows], x[k:k + half]]
        return [x, jnp.concatenate(turned, axis=0)]

    def apply(lhs, weight):
        return jnp.dot(lhs, weight.reshape(-1, width), preferred_element_type=F32)

    def gathered(block):
        return apply(
            jnp.concatenate(with_turned(block.reshape(2 * rows, width)), axis=1), forward_mem[core, me_block]
        )

    total = None
    for k in [0, 1, *range(2, n)]:
        me_block = lax.rem(me + k, n) if k != 1 else twin
        if k >= 2:
            me_block = 2 * chip_order[k // 2] + k % 2
        if k == 0:
            block = up_own[...]
        else:
            arrived(up_all.at[me_block], gather_rsem.at[me_block])
            block = up_all[me_block]
        term = gathered(block)
        total = term if total is None else total + term
    total = total.reshape(2, rows, width)
    up_send[0] = total.astype(BF16)

    @pl.when(has_above)
    def _():
        for q in far_chips:
            for h in range(2):
                up_step0(q, h).start()

    first_half, second_half = total[0], total[1]
    first_term[core] = jnp.where(core == 0, first_half, second_half)
    twin_term[...] = jnp.where(core == 0, second_half, first_half)
    give_term.start()

    def spread(blocks):
        sides = []
        for x in blocks:
            sides += with_turned(x)
        return jnp.concatenate(sides, axis=1)

    def send_down(t, out):
        for j in range(n):
            down_send[t, j] = out[j].astype(BF16)

        @pl.when(has_below)
        def _():
            for q in far_chips:
                down_step(t, q).start()

    @pl.when(has_above)
    def _():
        for h in range(2):
            arrived(first_in.at[h], first_rsem.at[h])

    lhs = spread([first_in[0], first_in[1]])
    for j in range(n):
        arrived(backward_mem.at[j, 1 - core], back_rsem.at[j])
    out = [apply(lhs, backward_mem[j]) for j in range(n)]
    for j in range(n):
        base[j] = out[j]
    send_down(0, out)

    for t in range(1, STEPS):
        last = t == STEPS - 1
        if t == 1:
            for j in range(n):
                arrived(forward_mem.at[1 - core, j], forw_rsem.at[j])
            arrived(first_term.at[1 - core], term_rsem)
        total = [first_term[h] for h in range(2)]
        for q in chip_order:

            @pl.when(has_below)
            def _():
                if t == 1:
                    for h in range(2):
                        arrived(up_in.at[0, 2 * q + h], up_rsem0.at[2 * q + h])
                else:
                    arrived(up_in.at[1, pl.ds(2 * q, 2)], up_rsem.at[q])

            lhs = spread([up_in[t - 1, 2 * q], up_in[t - 1, 2 * q + 1]])
            total = [
                total[h] + apply(lhs, forward_mem[h, pl.ds(2 * q, 2)]) for h in range(2)
            ]
        for h in range(2):
            if last:
                up_last_send[h] = total[h].astype(BF16)
            else:
                up_send[t, h] = total[h].astype(BF16)

        @pl.when(has_above)
        def _():
            if last:
                for h in range(2):
                    up_last(h).start()
            else:
                for q in far_chips:
                    up_step1(q).start()

        @pl.when(has_above)
        def _():
            for q in chip_order:
                arrived(down_in.at[t - 1, q], down_rsem.at[t - 1, q])

        blocks = []
        for h in range(2):
            x = down_in[t - 1, chip_order[0], h].astype(F32)
            for q in chip_order[1:]:
                x = x + down_in[t - 1, q, h].astype(F32)
            blocks.append(x.astype(BF16))
        lhs = spread(blocks)
        if not last:
            send_down(t, [base[j] + apply(lhs, backward_mem[j]) for j in range(n)])
        else:
            for k in far_first:
                to = lax.rem(me + k, n)
                down_last_send[to] = (base[to] + apply(lhs, backward_mem[to])).astype(BF16)
                down_last(k).start()
            own_part = base[me] + apply(lhs, backward_mem[me])

    def place(ref, halves):
        for h, x in enumerate(halves):
            for part in range(2):
                ref[0, part, h * half:(h + 1) * half] = x[part * half:(part + 1) * half].astype(BF16)

    halves = []
    for k in range(1, n):
        block = lax.rem(me + k, n)
        arrived(down_last_in.at[block], down_last_rsem.at[block])
    for h in range(2):
        x = down_own[h].astype(F32)
        for q in range(chips):
            block = 2 * q + h
            x = x + jnp.where(block == me, own_part, down_last_in[block].astype(F32))
        halves.append(x)
    place(down_out, halves)

    @pl.when(has_below)
    def _():
        for h in range(2):
            arrived(up_last_in.at[h], up_last_rsem.at[h])

    place(up_out, [up_own[h].astype(F32) + up_last_in[h].astype(F32) for h in range(2)])

    for k in range(1, n):
        gather(k).wait_send()
        down_last(k).wait_send()
    for j in range(n):
        give_backward(j).wait_send()
        give_forward(j).wait_send()
    give_term.wait_send()

    @pl.when(has_below)
    def _():
        for h in range(2):
            first(h).wait_send()
        for t in range(STEPS - 1):
            for q in range(chips):
                down_step(t, q).wait_send()

    @pl.when(has_above)
    def _():
        for q in range(chips):
            for h in range(2):
                up_step0(q, h).wait_send()
            up_step1(q).wait_send()
        for h in range(2):
            up_last(h).wait_send()


def hand_over(up_mem, down_mem, up_out, down_out, sems):
    stores = [
        pltpu.make_async_copy(mem, dst, sems.at[i])
        for i, (mem, dst) in enumerate([(up_mem, up_out), (down_mem, down_out)])
    ]
    for store in stores:
        store.start()
    for store in stores:
        store.wait()


def solution(mesh):
    layers, n = mesh.shape["gz"], mesh.shape["xy"]
    chips = n // 2

    def on_device(up_source, down_source, source_layer, u_factor, v_factor, block_rank):
        _, _, sources, width = up_source.shape
        max_rank = u_factor.shape[4]
        rows = sources
        piece = (rows, width)
        anywhere = pl.BlockSpec(memory_space=pl.ANY)
        hbm = pl.BlockSpec(memory_space=pltpu.HBM)
        vmem = pl.BlockSpec(memory_space=pltpu.VMEM)
        dma = pltpu.SemaphoreType.DMA
        traces = pl.pallas_call(
            functools.partial(kernel, layers, n),
            out_shape=(pltpu.VMEM(up_source.shape, BF16), pltpu.VMEM(down_source.shape, BF16)),
            in_specs=[hbm] * 6,
            out_specs=(vmem, vmem),
            scratch_shapes=[
                pltpu.VMEM((2, sources, width), BF16),
                pltpu.VMEM((2, sources, width), BF16),
                pltpu.VMEM((1, sources), jnp.int32),
                pltpu.SMEM(block_rank.shape, jnp.int32),
                pltpu.VMEM(u_factor.shape[2:], BF16),
                pltpu.VMEM(v_factor.shape[2:], BF16),
                pltpu.VMEM((2, *piece), BF16),
                pltpu.VMEM((2, *piece), BF16),
                pltpu.VMEM((n, 2, *piece), BF16),
                pltpu.VMEM((2, *piece), BF16),
                pltpu.VMEM((2, n, 2, width, width), BF16),
                pltpu.VMEM((n, 2, 2, width, width), BF16),
                pltpu.VMEM((2, *piece), F32),
                pltpu.VMEM(piece, F32),
                pltpu.VMEM((n, *piece), F32),
                pltpu.VMEM((STEPS - 1, n, *piece), BF16),
                pltpu.VMEM((STEPS - 1, 2, *piece), BF16),
                pltpu.VMEM((STEPS - 1, chips, 2, *piece), BF16),
                pltpu.VMEM((STEPS - 1, n, *piece), BF16),
                pltpu.VMEM((2, *piece), BF16),
                pltpu.VMEM((2, *piece), BF16),
                pltpu.VMEM((n, *piece), BF16),
                pltpu.VMEM((n, *piece), BF16),
                dma((4,)), dma((n,)), dma((n,)),
                dma((n,)), dma((n,)),
                dma((2,)), dma((2,)),
                dma((n,)), dma((n,)),
                dma((n,)), dma((n,)),
                dma, dma,
                dma((n,)), dma((n,)),
                dma((chips,)), dma((chips,)),
                dma((2,)), dma((2,)),
                dma((STEPS - 1, chips)), dma((STEPS - 1, chips)),
                dma((n,)), dma((n,)),
            ],
            compiler_params=pltpu.CompilerParams(collective_id=0, has_side_effects=True),
        )(up_source, down_source, source_layer.reshape(1, sources), u_factor, v_factor, block_rank)
        traces = [pltpu.with_memory_space_constraint(x, pltpu.VMEM) for x in traces]
        return pl.pallas_call(
            hand_over,
            out_shape=(
                jax.ShapeDtypeStruct(up_source.shape, BF16),
                jax.ShapeDtypeStruct(down_source.shape, BF16),
            ),
            in_specs=[vmem, vmem],
            out_specs=(anywhere, anywhere),
            scratch_shapes=[dma((2,))],
        )(*traces)

    in_specs = (
        P("gz", None, None, "xy"),
        P("gz", None, None, "xy"),
        P(),
        P("gz", "xy", None, None, None, None),
        P("gz", "xy", None, None, None, None),
        P("gz", "xy", None),
    )
    out_specs = (P("gz", None, None, "xy"), P("gz", None, None, "xy"))
    return jax.shard_map(
        on_device, mesh=mesh, in_specs=in_specs, out_specs=out_specs, check_vma=False
    )
```

time: 26.6 us -> 22 us (0.83)
  the two profiles are of different devices: /device:TPU:8 before, /device:TPU:0 now
where the time goes in v1:
time: 22 us; the launch traced here: 21.8 us
  Pallas kernels  21.2 us (96%)
  between operations  0.64 us (3%)
    pallas_call x1, Pallas kernels, on_device(): pl.pallas_call(functools.partial(kernel, layers, n), out_shape=(pltpu.VME...  20.5 us
    pallas_call x1, Pallas kernels, on_device(): pl.pallas_call(hand_over, out_shape=(jax.ShapeDtypeStruct(up_source.shape...  0.65 us

profile of v1, /device:TPU:0, one launch (start us, length us, event | category | flops | bytes accessed | tf_op | source)
XLA Modules:
  0.0 21.8 jit_solution(7919811602902020281)
XLA Ops:
  0.6 20.5 %shard_map.77 = (bf16[1,2,32,256]{3,2,1,0:T(8,128)(2,1)S(1)}, bf16[1,2,32,256]{3,2,1,0:T(8,128)(2,1)S(1)}) custom-call(bf16[1,2,32,256]{3,2,1,0:T(8,128)(2,1)} %up_hbm.1, bf16[1,2,32,256]{3,2,1,0:T(8,128)(2,1)} %down_hbm.1, s32[1,32]{1,0:T(1,128)} %bitcast.1, bf16[1,1,4,2,128,256]{5,4,3,2,1,0:T(8,128)(2,1)} %u_hbm.1, bf16[1,1,4,2,128,256]{5,4,3,2,1,0:T(8,128)(2,1)} %v_hbm.1, ...), custom_call_target="tpu_custom_call" | custom-call | tf_op jit(solution)/shard_map/pallas_call | solution.py:398
  21.2 0.6 %shard_map.78 = (bf16[1,2,32,256]{3,2,1,0:T(8,128)(2,1)}, bf16[1,2,32,256]{3,2,1,0:T(8,128)(2,1)}) custom-call(bf16[1,2,32,256]{3,2,1,0:T(8,128)(2,1)S(1)} %get-tuple-element.4.up_mem, bf16[1,2,32,256]{3,2,1,0:T(8,128)(2,1)S(1)} %get-tuple-element.5.down_mem), custom_call_target="tpu_custom_call" | custom-call | tf_op jit(solution)/shard_map/pallas_call | solution.py:442

commit v2 on v1

v2 whole, which is shorter than its diff:
```python
import functools

import jax
import jax.numpy as jnp
from jax import lax
from jax.experimental import pallas as pl
from jax.experimental.pallas import tpu as pltpu
from jax.sharding import PartitionSpec as P

STEPS = 3
MESH = pl.DeviceIdType.MESH
F32, BF16 = jnp.float32, jnp.bfloat16
UP, DOWN = 0, 1
LEFT, RIGHT = 0, 1
ORDER = ((UP, DOWN), (UP, DOWN), (UP, DOWN))


def kernel(
    layers, n, up_hbm, down_hbm, layer_hbm, u_hbm, v_hbm, rank_hbm, up_out, down_out,
    layer_ref, rank_ref, own, factors, up_all, first_in, dense, up_base, down_base,
    up_in, up_send, down_in, down_send, up_last_in, up_last_send, down_last_in, down_last_send,
    load_sem, factor_sem, twin_ssem, twin_rsem, gather_ssem, gather_rsem, first_ssem, first_rsem,
    up_ssem, up_rsem, up_last_ssem, up_last_rsem, down_ssem, down_rsem, down_last_ssem, down_last_rsem,
    ready_sem,
):
    layer = lax.axis_index("gz")
    me = lax.axis_index("xy")
    has_above = layer < layers - 1
    has_below = layer > 0
    chips = n // 2
    chip = me // 2
    core = lax.rem(me, 2)
    twin = me + 1 - 2 * core
    _, _, sources, width = own.shape
    half = sources // 2
    rows = 2 * half
    max_rank = factors.shape[4]
    step = max_rank // 4
    chip_order = [lax.rem(chip + k, chips) for k in range(chips)]
    far_chips = chip_order[1:]
    far_first = [*far_chips, chip]

    def remote(src, dst, ssem, rsem, to_layer, to_block):
        return pltpu.make_async_remote_copy(
            src_ref=src, dst_ref=dst, send_sem=ssem, recv_sem=rsem,
            device_id={"gz": to_layer, "xy": to_block}, device_id_type=MESH,
        )

    def arrived(ref, rsem):
        remote(ref, ref, gather_ssem, rsem, layer, me).wait_recv()

    def sent(ref, ssem):
        remote(ref, ref, ssem, twin_rsem, layer, me).wait_send()

    def tell(sem, to_layer, to_block):
        pl.semaphore_signal(
            sem, inc=1, device_id={"gz": to_layer, "xy": to_block}, device_id_type=MESH
        )

    barrier = pltpu.get_barrier_semaphore()

    @pl.when(has_above)
    def _():
        tell(barrier, layer + 1, me)
        tell(barrier, layer + 1, twin)

    for q in far_chips:
        for h in range(2):
            tell(barrier, layer, 2 * q + h)
    tell(barrier, layer, twin)

    def half_of(ref, h):
        return ref.at[0, :, pl.ds(pl.multiple_of(h * half, half), half)]

    load_factors = [
        pltpu.make_async_copy(hbm.at[0, 0], factors.at[core, kind], factor_sem)
        for kind, hbm in ((LEFT, u_hbm), (RIGHT, v_hbm))
    ]
    load_rank = pltpu.make_async_copy(rank_hbm, rank_ref, load_sem.at[0])
    load_layer = pltpu.make_async_copy(layer_hbm, layer_ref, load_sem.at[1])
    load_half = pltpu.make_async_copy(half_of(up_hbm, core), up_all.at[me], load_sem.at[2])
    load_own = [
        pltpu.make_async_copy(hbm.at[0], own.at[kind], load_sem.at[3]) for kind, hbm in ((UP, up_hbm), (DOWN, down_hbm))
    ]
    for load in (*load_factors, load_rank, load_layer, load_half, *load_own):
        load.start()

    @pl.when(jnp.logical_not(has_below))
    def _():
        up_in[...] = jnp.zeros_like(up_in)
        up_last_in[...] = jnp.zeros_like(up_last_in)

    @pl.when(jnp.logical_not(has_above))
    def _():
        first_in[...] = jnp.zeros_like(first_in)
        down_in[...] = jnp.zeros_like(down_in)

    pl.semaphore_wait(barrier, n - 1 + jnp.where(has_below, 2, 0))

    def gather(to, h):
        return remote(half_of(up_hbm, h), up_all.at[me], gather_ssem, gather_rsem.at[chip], layer, to)

    def first(h):
        return remote(
            half_of(down_hbm, h), first_in.at[core], first_ssem, first_rsem, layer - 1, 2 * chip + h
        )

    def give_left():
        slot = factors.at[core, LEFT]
        return remote(slot, slot, twin_ssem, twin_rsem, layer, twin)

    def give_right():
        return remote(v_hbm.at[0, 0], factors.at[core, RIGHT], twin_ssem, twin_rsem, layer, twin)

    def up_step(t, q):
        return remote(
            up_send.at[t], up_in.at[t, pl.ds(2 * chip, 2)], up_ssem, up_rsem.at[t, chip], layer + 1, 2 * q + core
        )

    def up_last(h):
        return remote(
            up_last_send.at[h], up_last_in.at[core], up_last_ssem, up_last_rsem, layer + 1, 2 * chip + h
        )

    def down_step(t, q):
        return remote(
            down_send.at[t, pl.ds(2 * q, 2)], down_in.at[t, chip], down_ssem, down_rsem.at[t],
            layer - 1, 2 * q + core,
        )

    def slot_of(to):
        return lax.rem(to - me + n, n) - 1

    def down_last(to):
        slot = slot_of(to)
        return remote(
            down_last_send.at[slot], down_last_in.at[n - 2 - slot], down_last_ssem, down_last_rsem, layer, to
        )

    @pl.when(has_below)
    def _():
        for h in range(2):
            first(h).start()
        tell(ready_sem, layer - 1, me)

    for q in far_chips:
        for h in range(2):
            gather(2 * q + h, h).start()
    gather(twin, 1 - core).start()
    give_right().start()

    def turned(x):
        middle = x.shape[0] // 2
        return jnp.concatenate([-x[middle:], x[:middle]], axis=0)

    def spread(blocks):
        return jnp.concatenate([side for x in blocks for side in (x, turned(x))], axis=1)

    def dot(lhs, weights):
        return jnp.dot(lhs, weights, preferred_element_type=F32)

    def stacked(row, kind, j):
        return factors[row, kind, j].reshape(2 * max_rank, width)

    def outer(a, b):
        pair = jnp.concatenate(
            [
                jnp.concatenate([b[:max_rank], -b[max_rank:]], axis=0),
                jnp.concatenate([b[max_rank:], b[:max_rank]], axis=0),
            ],
            axis=1,
        )
        product = lax.dot_general(a, pair, (((0,), (0,)), ((), ())), preferred_element_type=F32).astype(BF16)
        return product[:, :width], product[:, width:]

    def make_dense(row, kind):
        first_kind, second_kind = (RIGHT, LEFT) if kind == UP else (LEFT, RIGHT)
        for j in range(n):
            for part, x in enumerate(outer(stacked(row, first_kind, j), stacked(row, second_kind, j))):
                dense[row, kind, j, part] = x

    pltpu.make_async_copy(factors.at[core], factors.at[core], factor_sem).wait()
    load_rank.wait()
    for j in range(n):
        for part in range(2):
            for g in range(4):
                spot = pl.ds(g * step, step)
                piece = factors[core, LEFT, j, part, spot]
                factors[core, LEFT, j, part, spot] = jnp.where(
                    rank_ref[0, 0, j] > g, piece, jnp.zeros_like(piece)
                )
    give_left().start()
    make_dense(core, UP)
    make_dense(core, DOWN)

    load_layer.wait()
    square = (sources, sources)
    diagonal = lax.broadcasted_iota(jnp.int32, square, 0) == lax.broadcasted_iota(jnp.int32, square, 1)
    source_layer = jnp.sum(
        jnp.where(diagonal, jnp.broadcast_to(layer_ref[...], square), 0), axis=1, keepdims=True
    )
    source_layer = jnp.broadcast_to(source_layer, (sources, width))
    my_half = jnp.where(core == 0, source_layer[:half], source_layer[half:])
    my_half = jnp.concatenate([my_half, my_half], axis=0)
    load_half.wait()
    pltpu.make_async_copy(own, own, load_sem.at[3]).wait()

    arrived(factors.at[1 - core], twin_rsem)
    make_dense(1 - core, UP)
    make_dense(1 - core, DOWN)

    def rise(t):
        last = t == STEPS - 1
        total = [up_base[h] if t > 0 else None for h in range(2)]
        for i, q in enumerate(chip_order):
            if t == 0:
                pair = up_all.at[pl.ds(2 * q, 2)]
                arrived(up_all.at[twin] if i == 0 else pair, gather_rsem.at[q])
            else:
                pair = up_in.at[t - 1, pl.ds(2 * q, 2)]

                @pl.when(has_below)
                def _():
                    arrived(pair, up_rsem.at[t - 1, q])

            lhs = spread([pair[h].reshape(rows, width) for h in range(2)])
            for h in range(2):
                term = dot(lhs, dense[h, UP, pl.ds(2 * q, 2)].reshape(4 * width, width))
                total[h] = term if total[h] is None else total[h] + term
        for h in range(2):
            if t == 0:
                total[h] = jnp.where(layer >= my_half, total[h], 0.0)
            if last:
                up_last_send[h] = total[h].astype(BF16)
            else:
                up_send[t, h] = total[h].astype(BF16)

        @pl.when(has_above)
        def _():
            if t == 0:
                pl.semaphore_wait(ready_sem, 1)
            if last:
                for h in range(2):
                    up_last(h).start()
            else:
                for q in far_first:
                    up_step(t, q).start()

        if t == 0:
            for h in range(2):
                up_base[h] = total[h]

    def fall(t):
        last = t == STEPS - 1

        @pl.when(has_above)
        def _():
            if t == 0:
                arrived(first_in, first_rsem)
            else:
                arrived(down_in.at[t - 1], down_rsem.at[t - 1])

        blocks = []
        for h in range(2):
            if t == 0:
                x = jnp.where(layer + 1 <= my_half, first_in[h].reshape(rows, width).astype(F32), 0.0)
            else:
                x = down_in[t - 1, 0, h].astype(F32)
                for q in range(1, chips):
                    x = x + down_in[t - 1, q, h].astype(F32)
            blocks.append(x.astype(BF16))
        lhs = spread(blocks)

        def back(j):
            out = dot(
                lhs, jnp.concatenate([dense[h, DOWN, j].reshape(2 * width, width) for h in range(2)], axis=0)
            )
            if t == 0:
                down_base[j] = out
            else:
                out = down_base[j] + out
            return out

        if last:
            for q in far_chips:
                for h in range(2):
                    down_last_send[slot_of(2 * q + h)] = back(2 * q + h).astype(BF16)
            for q in far_chips:
                for h in range(2):
                    down_last(2 * q + h).start()
            down_last_send[slot_of(twin)] = back(twin).astype(BF16)
            mine = back(me)
            down_last(twin).start()
            return mine
        for q in far_first:
            for h in range(2):
                down_send[t, 2 * q + h] = back(2 * q + h).astype(BF16)

        @pl.when(has_below)
        def _():
            for q in far_first:
                down_step(t, q).start()
        return None

    for t, order in enumerate(ORDER):
        for which in order:
            if which == UP:
                rise(t)
            else:
                mine = fall(t)

    def active(kind, keep):
        return [jnp.where(keep, own[kind, part].astype(F32), 0.0) for part in range(2)]

    def place(ref, start, halves):
        for h, x in enumerate(halves):
            for part in range(2):
                spot = pl.ds(h * half, half)
                ref[0, part, spot] = (
                    start[part][h * half:(h + 1) * half] + x[part * half:(part + 1) * half]
                ).astype(BF16)

    def finish_up():
        @pl.when(has_below)
        def _():
            arrived(up_last_in, up_last_rsem)

        place(up_out, active(UP, layer >= source_layer), [up_last_in[h].astype(F32) for h in range(2)])

    def finish_down():
        arrived(down_last_in, down_last_rsem)
        same, other = mine, 0.0
        for k in range(n - 1):
            x = down_last_in[k].astype(F32)
            if k % 2:
                same = same + x
            else:
                other = other + x
        place(
            down_out, active(DOWN, layer <= source_layer),
            [jnp.where(core == 0, same, other), jnp.where(core == 0, other, same)],
        )

    finish_down()
    finish_up()

    sent(factors.at[core], twin_ssem)
    sent(down_last_send, gather_ssem)
    sent(down_last_send, down_last_ssem)

    @pl.when(has_below)
    def _():
        sent(first_in, first_ssem)
        sent(down_send, down_ssem)

    @pl.when(has_above)
    def _():
        sent(up_in, up_ssem)
        sent(up_last_send, up_last_ssem)


def hand_over(up_mem, down_mem, up_out, down_out, sems):
    stores = [
        pltpu.make_async_copy(mem, dst, sems.at[i])
        for i, (mem, dst) in enumerate([(up_mem, up_out), (down_mem, down_out)])
    ]
    for store in stores:
        store.start()
    for store in stores:
        store.wait()


def solution(mesh):
    layers, n = mesh.shape["gz"], mesh.shape["xy"]
    chips = n // 2

    def on_device(up_source, down_source, source_layer, u_factor, v_factor, block_rank):
        _, _, sources, width = up_source.shape
        half = sources // 2
        piece = (2 * half, width)
        anywhere = pl.BlockSpec(memory_space=pl.ANY)
        hbm = pl.BlockSpec(memory_space=pltpu.HBM)
        vmem = pl.BlockSpec(memory_space=pltpu.VMEM)
        dma = pltpu.SemaphoreType.DMA
        traces = pl.pallas_call(
            functools.partial(kernel, layers, n),
            out_shape=(pltpu.VMEM(up_source.shape, BF16), pltpu.VMEM(down_source.shape, BF16)),
            in_specs=[hbm] * 6,
            out_specs=(vmem, vmem),
            scratch_shapes=[
                pltpu.VMEM((1, sources), jnp.int32),
                pltpu.SMEM(block_rank.shape, jnp.int32),
                pltpu.VMEM((2, *up_source.shape[1:]), BF16),
                pltpu.VMEM((2, 2, *u_factor.shape[2:]), BF16),
                pltpu.VMEM((n, 2, half, width), BF16),
                pltpu.VMEM((2, 2, half, width), BF16),
                pltpu.VMEM((2, 2, n, 2, width, width), BF16),
                pltpu.VMEM((2, *piece), F32),
                pltpu.VMEM((n, *piece), F32),
                pltpu.VMEM((STEPS - 1, n, *piece), BF16),
                pltpu.VMEM((STEPS - 1, 2, *piece), BF16),
                pltpu.VMEM((STEPS - 1, chips, 2, *piece), BF16),
                pltpu.VMEM((STEPS - 1, n, *piece), BF16),
                pltpu.VMEM((2, *piece), BF16),
                pltpu.VMEM((2, *piece), BF16),
                pltpu.VMEM((n - 1, *piece), BF16),
                pltpu.VMEM((n - 1, *piece), BF16),
                dma((4,)), dma,
                dma, dma,
                dma, dma((chips,)),
                dma, dma,
                dma, dma((STEPS - 1, chips)),
                dma, dma,
                dma, dma((STEPS - 1,)),
                dma, dma,
                pltpu.SemaphoreType.REGULAR,
            ],
            compiler_params=pltpu.CompilerParams(collective_id=0, has_side_effects=True),
        )(up_source, down_source, source_layer.reshape(1, sources), u_factor, v_factor, block_rank)
        traces = [pltpu.with_memory_space_constraint(x, pltpu.VMEM) for x in traces]
        return pl.pallas_call(
            hand_over,
            out_shape=(
                jax.ShapeDtypeStruct(up_source.shape, BF16),
                jax.ShapeDtypeStruct(down_source.shape, BF16),
            ),
            in_specs=[vmem, vmem],
            out_specs=(anywhere, anywhere),
            scratch_shapes=[dma((2,))],
        )(*traces)

    in_specs = (
        P("gz", None, None, "xy"),
        P("gz", None, None, "xy"),
        P(),
        P("gz", "xy", None, None, None, None),
        P("gz", "xy", None, None, None, None),
        P("gz", "xy", None),
    )
    out_specs = (P("gz", None, None, "xy"), P("gz", None, None, "xy"))
    return jax.shard_map(
        on_device, mesh=mesh, in_specs=in_specs, out_specs=out_specs, check_vma=False
    )
```

time: 22 us -> 21.1 us (0.959)
  Pallas kernels: 21.2 us -> 20.3 us
    pallas_call x1, Pallas kernels: 20.5 us -> 19.6 us  [on_device(): pl.pallas_call(functools.partial(kernel, layers, n), out_shape=(pltpu.VME...]
where the time goes in v2:
time: 21.1 us; the launch traced here: 20.9 us
  Pallas kernels  20.3 us (96%)
  between operations  0.64 us (3%)
    pallas_call x1, Pallas kernels, on_device(): pl.pallas_call(functools.partial(kernel, layers, n), out_shape=(pltpu.VME...  19.6 us
    pallas_call x1, Pallas kernels, on_device(): pl.pallas_call(hand_over, out_shape=(jax.ShapeDtypeStruct(up_source.shape...  0.65 us

profile of v2, /device:TPU:0, one launch (start us, length us, event | category | flops | bytes accessed | tf_op | source)
XLA Modules:
  0.0 20.9 jit_solution(3473785703408342001)
XLA Ops:
  0.6 19.6 %shard_map.77 = (bf16[1,2,32,256]{3,2,1,0:T(8,128)(2,1)S(1)}, bf16[1,2,32,256]{3,2,1,0:T(8,128)(2,1)S(1)}) custom-call(bf16[1,2,32,256]{3,2,1,0:T(8,128)(2,1)} %up_hbm.1, bf16[1,2,32,256]{3,2,1,0:T(8,128)(2,1)} %down_hbm.1, s32[1,32]{1,0:T(1,128)} %bitcast.1, bf16[1,1,4,2,128,256]{5,4,3,2,1,0:T(8,128)(2,1)} %u_hbm.1, bf16[1,1,4,2,128,256]{5,4,3,2,1,0:T(8,128)(2,1)} %v_hbm.1, ...), custom_call_target="tpu_custom_call" | custom-call | tf_op jit(solution)/shard_map/pallas_call | solution.py:385
  20.3 0.6 %shard_map.78 = (bf16[1,2,32,256]{3,2,1,0:T(8,128)(2,1)}, bf16[1,2,32,256]{3,2,1,0:T(8,128)(2,1)}) custom-call(bf16[1,2,32,256]{3,2,1,0:T(8,128)(2,1)S(1)} %get-tuple-element.4.up_mem, bf16[1,2,32,256]{3,2,1,0:T(8,128)(2,1)S(1)} %get-tuple-element.5.down_mem), custom_call_target="tpu_custom_call" | custom-call | tf_op jit(solution)/shard_map/pallas_call | solution.py:421

commit v3 on v2

--- a/solution.py
+++ b/solution.py
@@ -30,6 +30,7 @@
     chips = n // 2
     chip = me // 2
     core = lax.rem(me, 2)
+    side = lax.rem(core + layer, 2)
     twin = me + 1 - 2 * core
     _, _, sources, width = own.shape
     half = sources // 2
@@ -50,7 +51,7 @@
         remote(ref, ref, gather_ssem, rsem, layer, me).wait_recv()
 
     def sent(ref, ssem):
-        remote(ref, ref, ssem, twin_rsem, layer, me).wait_send()
+        remote(ref, ref, ssem, twin_rsem.at[0], layer, me).wait_send()
 
     def tell(sem, to_layer, to_block):
         pl.semaphore_signal(
@@ -78,22 +79,35 @@
     ]
     load_rank = pltpu.make_async_copy(rank_hbm, rank_ref, load_sem.at[0])
     load_layer = pltpu.make_async_copy(layer_hbm, layer_ref, load_sem.at[1])
-    load_half = pltpu.make_async_copy(half_of(up_hbm, core), up_all.at[me], load_sem.at[2])
+    load_half = pltpu.make_async_copy(half_of(up_hbm, side), up_all.at[me], load_sem.at[2])
     load_own = [
         pltpu.make_async_copy(hbm.at[0], own.at[kind], load_sem.at[3]) for kind, hbm in ((UP, up_hbm), (DOWN, down_hbm))
     ]
     for load in (*load_factors, load_rank, load_layer, load_half, *load_own):
         load.start()
 
+    hears_up = jnp.logical_and(has_below, has_above)
+    feeds_up = layer < layers - 2
+    hears_down = [jnp.logical_and(has_below, feeds_up), feeds_up]
+    feeds_down = [jnp.logical_and(layer > 1, has_above), jnp.logical_and(has_below, has_above)]
+
+    @pl.when(jnp.logical_not(hears_up))
+    def _():
+        up_in[...] = jnp.zeros_like(up_in)
+
     @pl.when(jnp.logical_not(has_below))
     def _():
-        up_in[...] = jnp.zeros_like(up_in)
         up_last_in[...] = jnp.zeros_like(up_last_in)
 
     @pl.when(jnp.logical_not(has_above))
     def _():
         first_in[...] = jnp.zeros_like(first_in)
-        down_in[...] = jnp.zeros_like(down_in)
+
+    for t in range(STEPS - 1):
+
+        @pl.when(jnp.logical_not(hears_down[t]))
+        def _():
+            down_in[t] = jnp.zeros_like(down_in[t])
 
     pl.semaphore_wait(barrier, n - 1 + jnp.where(has_below, 2, 0))
 
@@ -102,30 +116,35 @@
 
     def first(h):
         return remote(
-            half_of(down_hbm, h), first_in.at[core], first_ssem, first_rsem, layer - 1, 2 * chip + h
-        )
-
-    def give_left():
-        slot = factors.at[core, LEFT]
-        return remote(slot, slot, twin_ssem, twin_rsem, layer, twin)
-
-    def give_right():
-        return remote(v_hbm.at[0, 0], factors.at[core, RIGHT], twin_ssem, twin_rsem, layer, twin)
+            half_of(down_hbm, lax.rem(layer + 1 + h, 2)), first_in.at[core], first_ssem, first_rsem, layer - 1, 2 * chip + h
+        )
+
+    def group(g):
+        return pl.ds(g * chips, chips)
+
+    def give_left(g):
+        slot = factors.at[core, LEFT, group(g)]
+        return remote(slot, slot, twin_ssem, twin_rsem.at[g], layer, twin)
+
+    def give_right(g):
+        return remote(
+            v_hbm.at[0, 0, group(g)], factors.at[core, RIGHT, group(g)], twin_ssem, twin_rsem.at[g], layer, twin
+        )
 
     def up_step(t, q):
         return remote(
-            up_send.at[t], up_in.at[t, pl.ds(2 * chip, 2)], up_ssem, up_rsem.at[t, chip], layer + 1, 2 * q + core
+            up_send.at[t], up_in.at[t, pl.ds(2 * chip, 2)], up_ssem, up_rsem.at[t, chip], layer + 1, 2 * q + 1 - core
         )
 
     def up_last(h):
         return remote(
-            up_last_send.at[h], up_last_in.at[core], up_last_ssem, up_last_rsem, layer + 1, 2 * chip + h
+            up_last_send.at[h], up_last_in.at[side], up_last_ssem, up_last_rsem, layer + 1, 2 * chip + h
         )
 
     def down_step(t, q):
         return remote(
-            down_send.at[t, pl.ds(2 * q, 2)], down_in.at[t, chip], down_ssem, down_rsem.at[t],
-            layer - 1, 2 * q + core,
+            down_send.at[t, pl.ds(2 * q, 2)], down_in.at[t, chip], down_ssem.at[t], down_rsem.at[t],
+            layer - 1, 2 * q + 1 - core,
         )
 
     def slot_of(to):
@@ -145,9 +164,10 @@
 
     for q in far_chips:
         for h in range(2):
-            gather(2 * q + h, h).start()
-    gather(twin, 1 - core).start()
-    give_right().start()
+            gather(2 * q + h, lax.rem(layer + h, 2)).start()
+    gather(twin, 1 - side).start()
+    for g in range(2):
+        give_right(g).start()
 
     def turned(x):
         middle = x.shape[0] // 2
@@ -173,9 +193,9 @@
         product = lax.dot_general(a, pair, (((0,), (0,)), ((), ())), preferred_element_type=F32).astype(BF16)
         return product[:, :width], product[:, width:]
 
-    def make_dense(row, kind):
+    def make_dense(row, kind, g):
         first_kind, second_kind = (RIGHT, LEFT) if kind == UP else (LEFT, RIGHT)
-        for j in range(n):
+        for j in range(g * chips, (g + 1) * chips):
             for part, x in enumerate(outer(stacked(row, first_kind, j), stacked(row, second_kind, j))):
                 dense[row, kind, j, part] = x
 
@@ -189,9 +209,11 @@
                 factors[core, LEFT, j, part, spot] = jnp.where(
                     rank_ref[0, 0, j] > g, piece, jnp.zeros_like(piece)
                 )
-    give_left().start()
-    make_dense(core, UP)
-    make_dense(core, DOWN)
+    for g in range(2):
+        give_left(g).start()
+    for g in range(2):
+        make_dense(core, UP, g)
+        make_dense(core, DOWN, g)
 
     load_layer.wait()
     square = (sources, sources)
@@ -200,14 +222,16 @@
         jnp.where(diagonal, jnp.broadcast_to(layer_ref[...], square), 0), axis=1, keepdims=True
     )
     source_layer = jnp.broadcast_to(source_layer, (sources, width))
-    my_half = jnp.where(core == 0, source_layer[:half], source_layer[half:])
+    my_half = jnp.where(side == 0, source_layer[:half], source_layer[half:])
     my_half = jnp.concatenate([my_half, my_half], axis=0)
     load_half.wait()
     pltpu.make_async_copy(own, own, load_sem.at[3]).wait()
 
-    arrived(factors.at[1 - core], twin_rsem)
-    make_dense(1 - core, UP)
-    make_dense(1 - core, DOWN)
+    for g in range(2):
+        arrived(factors.at[1 - core, :, group(g)], twin_rsem.at[g])
+        make_dense(1 - core, UP, g)
+        if g == 0:
+            make_dense(1 - core, DOWN, g)
 
     def rise(t):
         last = t == STEPS - 1
@@ -219,7 +243,7 @@
             else:
                 pair = up_in.at[t - 1, pl.ds(2 * q, 2)]
 
-                @pl.when(has_below)
+                @pl.when(hears_up)
                 def _():
                     arrived(pair, up_rsem.at[t - 1, q])
 
@@ -235,10 +259,14 @@
             else:
                 up_send[t, h] = total[h].astype(BF16)
 
-        @pl.when(has_above)
-        def _():
-            if t == 0:
+        if t == 0:
+
+            @pl.when(has_above)
+            def _():
                 pl.semaphore_wait(ready_sem, 1)
+
+        @pl.when(has_above if last else feeds_up)
+        def _():
             if last:
                 for h in range(2):
                     up_last(h).start()
@@ -252,8 +280,10 @@
 
     def fall(t):
         last = t == STEPS - 1
-
-        @pl.when(has_above)
+        if t == 0:
+            make_dense(1 - core, DOWN, 1)
+
+        @pl.when(has_above if t == 0 else hears_down[t - 1])
         def _():
             if t == 0:
                 arrived(first_in, first_rsem)
@@ -296,7 +326,7 @@
             for h in range(2):
                 down_send[t, 2 * q + h] = back(2 * q + h).astype(BF16)
 
-        @pl.when(has_below)
+        @pl.when(feeds_down[t])
         def _():
             for q in far_first:
                 down_step(t, q).start()
@@ -338,7 +368,7 @@
                 other = other + x
         place(
             down_out, active(DOWN, layer <= source_layer),
-            [jnp.where(core == 0, same, other), jnp.where(core == 0, other, same)],
+            [jnp.where(side == 0, same, other), jnp.where(side == 0, other, same)],
         )
 
     finish_down()
@@ -351,11 +381,19 @@
     @pl.when(has_below)
     def _():
         sent(first_in, first_ssem)
-        sent(down_send, down_ssem)
+
+    for t in range(STEPS - 1):
+
+        @pl.when(feeds_down[t])
+        def _():
+            sent(down_send.at[t], down_ssem.at[t])
+
+    @pl.when(feeds_up)
+    def _():
+        sent(up_in, up_ssem)
 
     @pl.when(has_above)
     def _():
-        sent(up_in, up_ssem)
         sent(up_last_send, up_last_ssem)
 
 
@@ -406,12 +444,12 @@
                 pltpu.VMEM((n - 1, *piece), BF16),
                 pltpu.VMEM((n - 1, *piece), BF16),
                 dma((4,)), dma,
-                dma, dma,
+                dma, dma((2,)),
                 dma, dma((chips,)),
                 dma, dma,
                 dma, dma((STEPS - 1, chips)),
                 dma, dma,
-                dma, dma((STEPS - 1,)),
+                dma((STEPS - 1,)), dma((STEPS - 1,)),
                 dma, dma,
                 pltpu.SemaphoreType.REGULAR,
             ],

time: 21.1 us -> 20.4 us (0.967)
  Pallas kernels: 20.3 us -> 19.6 us
    pallas_call x1, Pallas kernels: 19.6 us -> 19 us  [on_device(): pl.pallas_call(functools.partial(kernel, layers, n), out_shape=(pltpu.VME...]
where the time goes in v3:
time: 20.4 us; the launch traced here: 20.3 us
  Pallas kernels  19.6 us (96%)
  between operations  0.64 us (3%)
    pallas_call x1, Pallas kernels, on_device(): pl.pallas_call(functools.partial(kernel, layers, n), out_shape=(pltpu.VME...  19 us
    pallas_call x1, Pallas kernels, on_device(): pl.pallas_call(hand_over, out_shape=(jax.ShapeDtypeStruct(up_source.shape...  0.65 us

profile of v3, /device:TPU:0, one launch (start us, length us, event | category | flops | bytes accessed | tf_op | source)
XLA Modules:
  0.0 20.3 jit_solution(3600525355185681565)
XLA Ops:
  0.6 19.0 %shard_map.77 = (bf16[1,2,32,256]{3,2,1,0:T(8,128)(2,1)S(1)}, bf16[1,2,32,256]{3,2,1,0:T(8,128)(2,1)S(1)}) custom-call(bf16[1,2,32,256]{3,2,1,0:T(8,128)(2,1)} %up_hbm.1, bf16[1,2,32,256]{3,2,1,0:T(8,128)(2,1)} %down_hbm.1, s32[1,32]{1,0:T(1,128)} %bitcast.1, bf16[1,1,4,2,128,256]{5,4,3,2,1,0:T(8,128)(2,1)} %u_hbm.1, bf16[1,1,4,2,128,256]{5,4,3,2,1,0:T(8,128)(2,1)} %v_hbm.1, ...), custom_call_target="tpu_custom_call" | custom-call | tf_op jit(solution)/shard_map/pallas_call | solution.py:423
  19.6 0.6 %shard_map.78 = (bf16[1,2,32,256]{3,2,1,0:T(8,128)(2,1)}, bf16[1,2,32,256]{3,2,1,0:T(8,128)(2,1)}) custom-call(bf16[1,2,32,256]{3,2,1,0:T(8,128)(2,1)S(1)} %get-tuple-element.4.up_mem, bf16[1,2,32,256]{3,2,1,0:T(8,128)(2,1)S(1)} %get-tuple-element.5.down_mem), custom_call_target="tpu_custom_call" | custom-call | tf_op jit(solution)/shard_map/pallas_call | solution.py:459

commit v4 on v3

--- a/solution.py
+++ b/solution.py
@@ -12,16 +12,14 @@
 F32, BF16 = jnp.float32, jnp.bfloat16
 UP, DOWN = 0, 1
 LEFT, RIGHT = 0, 1
-ORDER = ((UP, DOWN), (UP, DOWN), (UP, DOWN))
 
 
 def kernel(
     layers, n, up_hbm, down_hbm, layer_hbm, u_hbm, v_hbm, rank_hbm, up_out, down_out,
     layer_ref, rank_ref, own, factors, up_all, first_in, dense, up_base, down_base,
-    up_in, up_send, down_in, down_send, up_last_in, up_last_send, down_last_in, down_last_send,
-    load_sem, factor_sem, twin_ssem, twin_rsem, gather_ssem, gather_rsem, first_ssem, first_rsem,
-    up_ssem, up_rsem, up_last_ssem, up_last_rsem, down_ssem, down_rsem, down_last_ssem, down_last_rsem,
-    ready_sem,
+    up_in, up_send, down_in, down_send, up_last_send, last, mine,
+    load_sem, factor_sem, twin_ssem, twin_rsem, gather_ssem, gather_rsem, first_rsem,
+    up_ssem, up_rsem, up_last_rsem, down_ssem, down_rsem, down_last_rsem, ready_sem,
 ):
     layer = lax.axis_index("gz")
     me = lax.axis_index("xy")
@@ -40,6 +38,8 @@
     chip_order = [lax.rem(chip + k, chips) for k in range(chips)]
     far_chips = chip_order[1:]
     far_first = [*far_chips, chip]
+    inner = (STEPS - 1) * n
+    last_in, last_send = last.at[0], last.at[1]
 
     def remote(src, dst, ssem, rsem, to_layer, to_block):
         return pltpu.make_async_remote_copy(
@@ -79,11 +79,10 @@
     ]
     load_rank = pltpu.make_async_copy(rank_hbm, rank_ref, load_sem.at[0])
     load_layer = pltpu.make_async_copy(layer_hbm, layer_ref, load_sem.at[1])
-    load_half = pltpu.make_async_copy(half_of(up_hbm, side), up_all.at[me], load_sem.at[2])
     load_own = [
-        pltpu.make_async_copy(hbm.at[0], own.at[kind], load_sem.at[3]) for kind, hbm in ((UP, up_hbm), (DOWN, down_hbm))
+        pltpu.make_async_copy(hbm.at[0], own.at[kind], load_sem.at[2]) for kind, hbm in ((UP, up_hbm), (DOWN, down_hbm))
     ]
-    for load in (*load_factors, load_rank, load_layer, load_half, *load_own):
+    for load in (*load_factors, load_rank, load_layer, *load_own):
         load.start()
 
     hears_up = jnp.logical_and(has_below, has_above)
@@ -93,11 +92,11 @@
 
     @pl.when(jnp.logical_not(hears_up))
     def _():
-        up_in[...] = jnp.zeros_like(up_in)
+        up_in[:inner] = jnp.zeros_like(up_in[:inner])
 
     @pl.when(jnp.logical_not(has_below))
     def _():
-        up_last_in[...] = jnp.zeros_like(up_last_in)
+        up_in[inner:] = jnp.zeros_like(up_in[inner:])
 
     @pl.when(jnp.logical_not(has_above))
     def _():
@@ -116,7 +115,7 @@
 
     def first(h):
         return remote(
-            half_of(down_hbm, lax.rem(layer + 1 + h, 2)), first_in.at[core], first_ssem, first_rsem, layer - 1, 2 * chip + h
+            half_of(down_hbm, lax.rem(layer + 1 + h, 2)), first_in.at[core], down_ssem, first_rsem, layer - 1, 2 * chip + h
         )
 
     def group(g):
@@ -133,17 +132,17 @@
 
     def up_step(t, q):
         return remote(
-            up_send.at[t], up_in.at[t, pl.ds(2 * chip, 2)], up_ssem, up_rsem.at[t, chip], layer + 1, 2 * q + 1 - core
+            up_send.at[t], up_in.at[pl.ds(t * n + 2 * chip, 2)], up_ssem, up_rsem.at[t, chip], layer + 1, 2 * q + 1 - core
         )
 
     def up_last(h):
         return remote(
-            up_last_send.at[h], up_last_in.at[side], up_last_ssem, up_last_rsem, layer + 1, 2 * chip + h
-        )
-
-    def down_step(t, q):
-        return remote(
-            down_send.at[t, pl.ds(2 * q, 2)], down_in.at[t, chip], down_ssem.at[t], down_rsem.at[t],
+            up_last_send.at[h], up_in.at[inner + side], up_ssem, up_last_rsem, layer + 1, 2 * chip + h
+        )
+
+    def down_step(t, q, h):
+        return remote(
+            down_send.at[t * n + 2 * q + h], down_in.at[t, chip, h], down_ssem, down_rsem.at[t, h],
             layer - 1, 2 * q + 1 - core,
         )
 
@@ -153,7 +152,7 @@
     def down_last(to):
         slot = slot_of(to)
         return remote(
-            down_last_send.at[slot], down_last_in.at[n - 2 - slot], down_last_ssem, down_last_rsem, layer, to
+            last_send.at[slot], last_in.at[n - 2 - slot], gather_ssem, down_last_rsem, layer, to
         )
 
     @pl.when(has_below)
@@ -224,8 +223,8 @@
     source_layer = jnp.broadcast_to(source_layer, (sources, width))
     my_half = jnp.where(side == 0, source_layer[:half], source_layer[half:])
     my_half = jnp.concatenate([my_half, my_half], axis=0)
-    load_half.wait()
-    pltpu.make_async_copy(own, own, load_sem.at[3]).wait()
+    pltpu.make_async_copy(own, own, load_sem.at[2]).wait()
+    up_all[me] = jnp.where(side == 0, own[UP, :, :half], own[UP, :, half:])
 
     for g in range(2):
         arrived(factors.at[1 - core, :, group(g)], twin_rsem.at[g])
@@ -233,15 +232,27 @@
         if g == 0:
             make_dense(1 - core, DOWN, g)
 
+    def send_up(t):
+        is_last = t == STEPS - 1
+
+        @pl.when(has_above if is_last else feeds_up)
+        def _():
+            if is_last:
+                for h in range(2):
+                    up_last(h).start()
+            else:
+                for q in far_first:
+                    up_step(t, q).start()
+
     def rise(t):
-        last = t == STEPS - 1
+        is_last = t == STEPS - 1
         total = [up_base[h] if t > 0 else None for h in range(2)]
-        for i, q in enumerate(chip_order):
+        for i, q in enumerate(chip_order if t == 0 else chip_order):
             if t == 0:
                 pair = up_all.at[pl.ds(2 * q, 2)]
                 arrived(up_all.at[twin] if i == 0 else pair, gather_rsem.at[q])
             else:
-                pair = up_in.at[t - 1, pl.ds(2 * q, 2)]
+                pair = up_in.at[pl.ds((t - 1) * n + 2 * q, 2)]
 
                 @pl.when(hears_up)
                 def _():
@@ -254,7 +265,7 @@
         for h in range(2):
             if t == 0:
                 total[h] = jnp.where(layer >= my_half, total[h], 0.0)
-            if last:
+            if is_last:
                 up_last_send[h] = total[h].astype(BF16)
             else:
                 up_send[t, h] = total[h].astype(BF16)
@@ -265,79 +276,75 @@
             def _():
                 pl.semaphore_wait(ready_sem, 1)
 
-        @pl.when(has_above if last else feeds_up)
-        def _():
-            if last:
-                for h in range(2):
-                    up_last(h).start()
-            else:
-                for q in far_first:
-                    up_step(t, q).start()
-
         if t == 0:
             for h in range(2):
                 up_base[h] = total[h]
+        send_up(t)
 
     def fall(t):
-        last = t == STEPS - 1
+        is_last = t == STEPS - 1
         if t == 0:
             make_dense(1 - core, DOWN, 1)
 
-        @pl.when(has_above if t == 0 else hears_down[t - 1])
-        def _():
-            if t == 0:
+        if t == 0:
+
+            @pl.when(has_above)
+            def _():
                 arrived(first_in, first_rsem)
-            else:
-                arrived(down_in.at[t - 1], down_rsem.at[t - 1])
-
-        blocks = []
+
+        lhs = []
+        blocks = [2 * q + h for q in far_first for h in range(2)]
+        partial = {}
         for h in range(2):
             if t == 0:
                 x = jnp.where(layer + 1 <= my_half, first_in[h].reshape(rows, width).astype(F32), 0.0)
             else:
+
+                @pl.when(hears_down[t - 1])
+                def _():
+                    arrived(down_in.at[t - 1, :, h], down_rsem.at[t - 1, h])
+
                 x = down_in[t - 1, 0, h].astype(F32)
                 for q in range(1, chips):
                     x = x + down_in[t - 1, q, h].astype(F32)
-            blocks.append(x.astype(BF16))
-        lhs = spread(blocks)
-
-        def back(j):
-            out = dot(
-                lhs, jnp.concatenate([dense[h, DOWN, j].reshape(2 * width, width) for h in range(2)], axis=0)
-            )
+            lhs.append(spread([x.astype(BF16)]))
+            if t > 0 and h == 0:
+                for i, j in enumerate(blocks):
+                    partial[i] = down_base[j] + dot(lhs[0], dense[0, DOWN, j].reshape(2 * width, width))
+
+        def back(i):
+            j = blocks[i]
             if t == 0:
+                out = dot(
+                    jnp.concatenate(lhs, axis=1),
+                    jnp.concatenate([dense[h, DOWN, j].reshape(2 * width, width) for h in range(2)], axis=0),
+                )
                 down_base[j] = out
-            else:
-                out = down_base[j] + out
-            return out
-
-        if last:
-            for q in far_chips:
-                for h in range(2):
-                    down_last_send[slot_of(2 * q + h)] = back(2 * q + h).astype(BF16)
-            for q in far_chips:
-                for h in range(2):
-                    down_last(2 * q + h).start()
-            down_last_send[slot_of(twin)] = back(twin).astype(BF16)
-            mine = back(me)
+                return out
+            return partial[i] + dot(lhs[1], dense[1, DOWN, j].reshape(2 * width, width))
+
+        if is_last:
+            for i in range(n - 2):
+                last_send[slot_of(blocks[i])] = back(i).astype(BF16)
+            for i in range(n - 2):
+                down_last(blocks[i]).start()
+            near = [back(n - 2), back(n - 1)]
+            last_send[slot_of(twin)] = jnp.where(core == 0, near[1], near[0]).astype(BF16)
             down_last(twin).start()
-            return mine
-        for q in far_first:
-            for h in range(2):
-                down_send[t, 2 * q + h] = back(2 * q + h).astype(BF16)
+            mine[...] = jnp.where(core == 0, near[0], near[1])
+            return
+        for i in range(n):
+            down_send[t * n + blocks[i]] = back(i).astype(BF16)
 
         @pl.when(feeds_down[t])
         def _():
             for q in far_first:
-                down_step(t, q).start()
-        return None
-
-    for t, order in enumerate(ORDER):
-        for which in order:
-            if which == UP:
-                rise(t)
-            else:
-                mine = fall(t)
+                for h in range(2):
+                    down_step(t, q, h).start()
+
+    for t in range(STEPS):
+        rise(t)
+        fall(t)
 
     def active(kind, keep):
         return [jnp.where(keep, own[kind, part].astype(F32), 0.0) for part in range(2)]
@@ -353,15 +360,15 @@
     def finish_up():
         @pl.when(has_below)
         def _():
-            arrived(up_last_in, up_last_rsem)
-
-        place(up_out, active(UP, layer >= source_layer), [up_last_in[h].astype(F32) for h in range(2)])
+            arrived(up_in.at[pl.ds(inner, 2)], up_last_rsem)
+
+        place(up_out, active(UP, layer >= source_layer), [up_in[inner + h].astype(F32) for h in range(2)])
 
     def finish_down():
-        arrived(down_last_in, down_last_rsem)
-        same, other = mine, 0.0
+        arrived(last_in, down_last_rsem)
+        same, other = mine[...], 0.0
         for k in range(n - 1):
-            x = down_last_in[k].astype(F32)
+            x = last_in[k].astype(F32)
             if k % 2:
                 same = same + x
             else:
@@ -375,26 +382,18 @@
     finish_up()
 
     sent(factors.at[core], twin_ssem)
-    sent(down_last_send, gather_ssem)
-    sent(down_last_send, down_last_ssem)
-
-    @pl.when(has_below)
-    def _():
-        sent(first_in, first_ssem)
-
-    for t in range(STEPS - 1):
-
-        @pl.when(feeds_down[t])
+    sent(last, gather_ssem)
+
+    def sent_when(condition, buffer, pieces, ssem):
+        @pl.when(condition)
         def _():
-            sent(down_send.at[t], down_ssem.at[t])
-
-    @pl.when(feeds_up)
-    def _():
-        sent(up_in, up_ssem)
-
-    @pl.when(has_above)
-    def _():
-        sent(up_last_send, up_last_ssem)
+            sent(buffer.at[pl.ds(0, pieces)], ssem)
+
+    sent_when(feeds_up, up_in, inner + 2, up_ssem)
+    sent_when(layer == layers - 2, up_in, 2, up_ssem)
+    sent_when(feeds_down[0], down_send, inner + 2, down_ssem)
+    sent_when(jnp.logical_and(layer == 1, has_above), down_send, inner + 2 - n, down_ssem)
+    sent_when(jnp.logical_and(has_below, jnp.logical_not(has_above)), down_send, 2, down_ssem)
 
 
 def hand_over(up_mem, down_mem, up_out, down_out, sems):
@@ -435,22 +434,18 @@
                 pltpu.VMEM((2, 2, n, 2, width, width), BF16),
                 pltpu.VMEM((2, *piece), F32),
                 pltpu.VMEM((n, *piece), F32),
-                pltpu.VMEM((STEPS - 1, n, *piece), BF16),
+                pltpu.VMEM(((STEPS - 1) * n + 2, *piece), BF16),
                 pltpu.VMEM((STEPS - 1, 2, *piece), BF16),
                 pltpu.VMEM((STEPS - 1, chips, 2, *piece), BF16),
-                pltpu.VMEM((STEPS - 1, n, *piece), BF16),
+                pltpu.VMEM(((STEPS - 1) * n + 2, *piece), BF16),
                 pltpu.VMEM((2, *piece), BF16),
-                pltpu.VMEM((2, *piece), BF16),
-                pltpu.VMEM((n - 1, *piece), BF16),
-                pltpu.VMEM((n - 1, *piece), BF16),
-                dma((4,)), dma,
+                pltpu.VMEM((2, n - 1, *piece), BF16),
+                pltpu.VMEM(piece, F32),
+                dma((3,)), dma,
                 dma, dma((2,)),
-                dma, dma((chips,)),
-                dma, dma,
-                dma, dma((STEPS - 1, chips)),
-                dma, dma,
-                dma((STEPS - 1,)), dma((STEPS - 1,)),
-                dma, dma,
+                dma, dma((chips,)), dma,
+                dma, dma((STEPS - 1, chips)), dma,
+                dma, dma((STEPS - 1, 2)), dma,
                 pltpu.SemaphoreType.REGULAR,
             ],
             compiler_params=pltpu.CompilerParams(collective_id=0, has_side_effects=True),

time: 20.4 us -> 20.1 us (0.985)
  Pallas kernels: 19.6 us -> 19.3 us
    pallas_call x1, Pallas kernels: 19 us -> 18.7 us  [on_device(): pl.pallas_call(functools.partial(kernel, layers, n), out_shape=(pltpu.VME...]
where the time goes in v4:
time: 20.1 us; the launch traced here: 20 us
  Pallas kernels  19.3 us (96%)
  between operations  0.64 us (3%)
    pallas_call x1, Pallas kernels, on_device(): pl.pallas_call(functools.partial(kernel, layers, n), out_shape=(pltpu.VME...  18.7 us
    pallas_call x1, Pallas kernels, on_device(): pl.pallas_call(hand_over, out_shape=(jax.ShapeDtypeStruct(up_source.shape...  0.65 us

profile of v4, /device:TPU:0, one launch (start us, length us, event | category | flops | bytes accessed | tf_op | source)
XLA Modules:
  0.0 20.0 jit_solution(12636234564166379812)
XLA Ops:
  0.6 18.7 %shard_map.77 = (bf16[1,2,32,256]{3,2,1,0:T(8,128)(2,1)S(1)}, bf16[1,2,32,256]{3,2,1,0:T(8,128)(2,1)S(1)}) custom-call(bf16[1,2,32,256]{3,2,1,0:T(8,128)(2,1)} %up_hbm.1, bf16[1,2,32,256]{3,2,1,0:T(8,128)(2,1)} %down_hbm.1, s32[1,32]{1,0:T(1,128)} %bitcast.1, bf16[1,1,4,2,128,256]{5,4,3,2,1,0:T(8,128)(2,1)} %u_hbm.1, bf16[1,1,4,2,128,256]{5,4,3,2,1,0:T(8,128)(2,1)} %v_hbm.1, ...), custom_call_target="tpu_custom_call" | custom-call | tf_op jit(solution)/shard_map/pallas_call | solution.py:422
  19.3 0.6 %shard_map.78 = (bf16[1,2,32,256]{3,2,1,0:T(8,128)(2,1)}, bf16[1,2,32,256]{3,2,1,0:T(8,128)(2,1)}) custom-call(bf16[1,2,32,256]{3,2,1,0:T(8,128)(2,1)S(1)} %get-tuple-element.4.up_mem, bf16[1,2,32,256]{3,2,1,0:T(8,128)(2,1)S(1)} %get-tuple-element.5.down_mem), custom_call_target="tpu_custom_call" | custom-call | tf_op jit(solution)/shard_map/pallas_call | solution.py:454

commit v5 on v4

--- a/solution.py
+++ b/solution.py
@@ -118,8 +118,11 @@
             half_of(down_hbm, lax.rem(layer + 1 + h, 2)), first_in.at[core], down_ssem, first_rsem, layer - 1, 2 * chip + h
         )
 
+    groups = n
+    size = n // groups
+
     def group(g):
-        return pl.ds(g * chips, chips)
+        return pl.ds(g * size, size)
 
     def give_left(g):
         slot = factors.at[core, LEFT, group(g)]
@@ -154,6 +157,10 @@
         return remote(
             last_send.at[slot], last_in.at[n - 2 - slot], gather_ssem, down_last_rsem, layer, to
         )
+
+    for q in far_chips:
+        for h in range(2):
+            gather(2 * q + h, lax.rem(layer + h, 2)).start()
 
     @pl.when(has_below)
     def _():
@@ -161,12 +168,8 @@
             first(h).start()
         tell(ready_sem, layer - 1, me)
 
-    for q in far_chips:
-        for h in range(2):
-            gather(2 * q + h, lax.rem(layer + h, 2)).start()
     gather(twin, 1 - side).start()
-    for g in range(2):
-        give_right(g).start()
+    give_right(0).start()
 
     def turned(x):
         middle = x.shape[0] // 2
@@ -194,7 +197,7 @@
 
     def make_dense(row, kind, g):
         first_kind, second_kind = (RIGHT, LEFT) if kind == UP else (LEFT, RIGHT)
-        for j in range(g * chips, (g + 1) * chips):
+        for j in range(g * size, (g + 1) * size):
             for part, x in enumerate(outer(stacked(row, first_kind, j), stacked(row, second_kind, j))):
                 dense[row, kind, j, part] = x
 
@@ -208,9 +211,11 @@
                 factors[core, LEFT, j, part, spot] = jnp.where(
                     rank_ref[0, 0, j] > g, piece, jnp.zeros_like(piece)
                 )
-    for g in range(2):
+    give_left(0).start()
+    for g in range(1, groups):
+        give_right(g).start()
         give_left(g).start()
-    for g in range(2):
+    for g in range(groups):
         make_dense(core, UP, g)
         make_dense(core, DOWN, g)
 
@@ -226,10 +231,10 @@
     pltpu.make_async_copy(own, own, load_sem.at[2]).wait()
     up_all[me] = jnp.where(side == 0, own[UP, :, :half], own[UP, :, half:])
 
-    for g in range(2):
+    for g in range(groups):
         arrived(factors.at[1 - core, :, group(g)], twin_rsem.at[g])
         make_dense(1 - core, UP, g)
-        if g == 0:
+        if g < groups - 1:
             make_dense(1 - core, DOWN, g)
 
     def send_up(t):
@@ -284,7 +289,7 @@
     def fall(t):
         is_last = t == STEPS - 1
         if t == 0:
-            make_dense(1 - core, DOWN, 1)
+            make_dense(1 - core, DOWN, groups - 1)
 
         if t == 0:
 
@@ -338,8 +343,8 @@
 
         @pl.when(feeds_down[t])
         def _():
-            for q in far_first:
-                for h in range(2):
+            for h in range(2):
+                for q in far_first:
                     down_step(t, q, h).start()
 
     for t in range(STEPS):
@@ -362,7 +367,7 @@
         def _():
             arrived(up_in.at[pl.ds(inner, 2)], up_last_rsem)
 
-        place(up_out, active(UP, layer >= source_layer), [up_in[inner + h].astype(F32) for h in range(2)])
+        place(up_out, active_up, [up_in[inner + h].astype(F32) for h in range(2)])
 
     def finish_down():
         arrived(last_in, down_last_rsem)
@@ -374,12 +379,14 @@
             else:
                 other = other + x
         place(
-            down_out, active(DOWN, layer <= source_layer),
+            down_out, active_down,
             [jnp.where(side == 0, same, other), jnp.where(side == 0, other, same)],
         )
 
+    active_up = active(UP, layer >= source_layer)
+    active_down = active(DOWN, layer <= source_layer)
+    finish_up()
     finish_down()
-    finish_up()
 
     sent(factors.at[core], twin_ssem)
     sent(last, gather_ssem)
@@ -442,7 +449,7 @@
                 pltpu.VMEM((2, n - 1, *piece), BF16),
                 pltpu.VMEM(piece, F32),
                 dma((3,)), dma,
-                dma, dma((2,)),
+                dma, dma((n,)),
                 dma, dma((chips,)), dma,
                 dma, dma((STEPS - 1, chips)), dma,
                 dma, dma((STEPS - 1, 2)), dma,

time: 20.1 us -> 19.9 us (0.990)
  no operation moved by 1% of the time
where the time goes in v5:
time: 19.9 us; the launch traced here: 19.8 us
  Pallas kernels  19.1 us (96%)
  between operations  0.64 us (3%)
    pallas_call x1, Pallas kernels, on_device(): pl.pallas_call(functools.partial(kernel, layers, n), out_shape=(pltpu.VME...  18.5 us
    pallas_call x1, Pallas kernels, on_device(): pl.pallas_call(hand_over, out_shape=(jax.ShapeDtypeStruct(up_source.shape...  0.65 us

profile of v5, /device:TPU:0, one launch (start us, length us, event | category | flops | bytes accessed | tf_op | source)
XLA Modules:
  0.0 19.8 jit_solution(3002851750187558946)
XLA Ops:
  0.6 18.5 %shard_map.77 = (bf16[1,2,32,256]{3,2,1,0:T(8,128)(2,1)S(1)}, bf16[1,2,32,256]{3,2,1,0:T(8,128)(2,1)S(1)}) custom-call(bf16[1,2,32,256]{3,2,1,0:T(8,128)(2,1)} %up_hbm.1, bf16[1,2,32,256]{3,2,1,0:T(8,128)(2,1)} %down_hbm.1, s32[1,32]{1,0:T(1,128)} %bitcast.1, bf16[1,1,4,2,128,256]{5,4,3,2,1,0:T(8,128)(2,1)} %u_hbm.1, bf16[1,1,4,2,128,256]{5,4,3,2,1,0:T(8,128)(2,1)} %v_hbm.1, ...), custom_call_target="tpu_custom_call" | custom-call | tf_op jit(solution)/shard_map/pallas_call | solution.py:429
  19.1 0.6 %shard_map.78 = (bf16[1,2,32,256]{3,2,1,0:T(8,128)(2,1)}, bf16[1,2,32,256]{3,2,1,0:T(8,128)(2,1)}) custom-call(bf16[1,2,32,256]{3,2,1,0:T(8,128)(2,1)S(1)} %get-tuple-element.4.up_mem, bf16[1,2,32,256]{3,2,1,0:T(8,128)(2,1)S(1)} %get-tuple-element.5.down_mem), custom_call_target="tpu_custom_call" | custom-call | tf_op jit(solution)/shard_map/pallas_call | solution.py:461

commit v6 on v5

--- a/solution.py
+++ b/solution.py
@@ -246,7 +246,7 @@
                 for h in range(2):
                     up_last(h).start()
             else:
-                for q in far_first:
+                for q in [jnp.where(core == 0, a, b) for a, b in zip(far_first, chip_order)]:
                     up_step(t, q).start()
 
     def rise(t):
@@ -281,10 +281,10 @@
             def _():
                 pl.semaphore_wait(ready_sem, 1)
 
+        send_up(t)
         if t == 0:
             for h in range(2):
                 up_base[h] = total[h]
-        send_up(t)
 
     def fall(t):
         is_last = t == STEPS - 1
@@ -314,16 +314,18 @@
                     x = x + down_in[t - 1, q, h].astype(F32)
             lhs.append(spread([x.astype(BF16)]))
             if t > 0 and h == 0:
-                for i, j in enumerate(blocks):
+                for i, j in enumerate(blocks[:n - 2] if is_last else blocks):
                     partial[i] = down_base[j] + dot(lhs[0], dense[0, DOWN, j].reshape(2 * width, width))
 
         def back(i):
             j = blocks[i]
-            if t == 0:
+            if i not in partial:
                 out = dot(
                     jnp.concatenate(lhs, axis=1),
                     jnp.concatenate([dense[h, DOWN, j].reshape(2 * width, width) for h in range(2)], axis=0),
                 )
+                if t > 0:
+                    return down_base[j] + out
                 down_base[j] = out
                 return out
             return partial[i] + dot(lhs[1], dense[1, DOWN, j].reshape(2 * width, width))

time: 19.9 us -> 19.9 us (level)
  no operation moved by 1% of the time
where the time goes in v6:
time: 19.9 us; the launch traced here: 19.8 us
  Pallas kernels  19.1 us (96%)
  between operations  0.64 us (3%)
    pallas_call x1, Pallas kernels, on_device(): pl.pallas_call(functools.partial(kernel, layers, n), out_shape=(pltpu.VME...  18.5 us
    pallas_call x1, Pallas kernels, on_device(): pl.pallas_call(hand_over, out_shape=(jax.ShapeDtypeStruct(up_source.shape...  0.65 us

profile of v6, /device:TPU:0, one launch (start us, length us, event | category | flops | bytes accessed | tf_op | source)
XLA Modules:
  0.0 19.8 jit_solution(13011307617818411917)
XLA Ops:
  0.6 18.5 %shard_map.77 = (bf16[1,2,32,256]{3,2,1,0:T(8,128)(2,1)S(1)}, bf16[1,2,32,256]{3,2,1,0:T(8,128)(2,1)S(1)}) custom-call(bf16[1,2,32,256]{3,2,1,0:T(8,128)(2,1)} %up_hbm.1, bf16[1,2,32,256]{3,2,1,0:T(8,128)(2,1)} %down_hbm.1, s32[1,32]{1,0:T(1,128)} %bitcast.1, bf16[1,1,4,2,128,256]{5,4,3,2,1,0:T(8,128)(2,1)} %u_hbm.1, bf16[1,1,4,2,128,256]{5,4,3,2,1,0:T(8,128)(2,1)} %v_hbm.1, ...), custom_call_target="tpu_custom_call" | custom-call | tf_op jit(solution)/shard_map/pallas_call | solution.py:431
  19.1 0.6 %shard_map.78 = (bf16[1,2,32,256]{3,2,1,0:T(8,128)(2,1)}, bf16[1,2,32,256]{3,2,1,0:T(8,128)(2,1)}) custom-call(bf16[1,2,32,256]{3,2,1,0:T(8,128)(2,1)S(1)} %get-tuple-element.4.up_mem, bf16[1,2,32,256]{3,2,1,0:T(8,128)(2,1)S(1)} %get-tuple-element.5.down_mem), custom_call_target="tpu_custom_call" | custom-call | tf_op jit(solution)/shard_map/pallas_call | solution.py:463

commit v7 on v6

--- a/solution.py
+++ b/solution.py
@@ -85,14 +85,17 @@
     for load in (*load_factors, load_rank, load_layer, *load_own):
         load.start()
 
-    hears_up = jnp.logical_and(has_below, has_above)
-    feeds_up = layer < layers - 2
-    hears_down = [jnp.logical_and(has_below, feeds_up), feeds_up]
+    feeds_up = [layer < layers - STEPS + t for t in range(STEPS)]
+    hears_up = [jnp.logical_and(has_below, layer - 1 < layers - STEPS + t) for t in range(STEPS - 1)]
+    low = layer < layers - 2
+    hears_down = [jnp.logical_and(has_below, low), low]
     feeds_down = [jnp.logical_and(layer > 1, has_above), jnp.logical_and(has_below, has_above)]
 
-    @pl.when(jnp.logical_not(hears_up))
-    def _():
-        up_in[:inner] = jnp.zeros_like(up_in[:inner])
+    for t in range(STEPS - 1):
+
+        @pl.when(jnp.logical_not(hears_up[t]))
+        def _():
+            up_in[t * n:(t + 1) * n] = jnp.zeros_like(up_in[t * n:(t + 1) * n])
 
     @pl.when(jnp.logical_not(has_below))
     def _():
@@ -240,13 +243,13 @@
     def send_up(t):
         is_last = t == STEPS - 1
 
-        @pl.when(has_above if is_last else feeds_up)
+        @pl.when(feeds_up[t])
         def _():
             if is_last:
                 for h in range(2):
                     up_last(h).start()
             else:
-                for q in [jnp.where(core == 0, a, b) for a, b in zip(far_first, chip_order)]:
+                for q in far_first:
                     up_step(t, q).start()
 
     def rise(t):
@@ -259,7 +262,7 @@
             else:
                 pair = up_in.at[pl.ds((t - 1) * n + 2 * q, 2)]
 
-                @pl.when(hears_up)
+                @pl.when(hears_up[t - 1])
                 def _():
                     arrived(pair, up_rsem.at[t - 1, q])
 
@@ -299,7 +302,7 @@
 
         lhs = []
         blocks = [2 * q + h for q in far_first for h in range(2)]
-        partial = {}
+        partial, fresh = {}, {}
         for h in range(2):
             if t == 0:
                 x = jnp.where(layer + 1 <= my_half, first_in[h].reshape(rows, width).astype(F32), 0.0)
@@ -326,7 +329,7 @@
                 )
                 if t > 0:
                     return down_base[j] + out
-                down_base[j] = out
+                fresh[i] = out
                 return out
             return partial[i] + dot(lhs[1], dense[1, DOWN, j].reshape(2 * width, width))
 
@@ -349,6 +352,9 @@
                 for q in far_first:
                     down_step(t, q, h).start()
 
+        for i, out in fresh.items():
+            down_base[blocks[i]] = out
+
     for t in range(STEPS):
         rise(t)
         fall(t)
@@ -398,8 +404,9 @@
         def _():
             sent(buffer.at[pl.ds(0, pieces)], ssem)
 
-    sent_when(feeds_up, up_in, inner + 2, up_ssem)
-    sent_when(layer == layers - 2, up_in, 2, up_ssem)
+    for t in range(STEPS):
+        began = feeds_up[0] if t == 0 else jnp.logical_and(feeds_up[t], jnp.logical_not(feeds_up[t - 1]))
+        sent_when(began, up_in, inner + 2 - t * n, up_ssem)
     sent_when(feeds_down[0], down_send, inner + 2, down_ssem)
     sent_when(jnp.logical_and(layer == 1, has_above), down_send, inner + 2 - n, down_ssem)
     sent_when(jnp.logical_and(has_below, jnp.logical_not(has_above)), down_send, 2, down_ssem)

time: 19.9 us -> 19.9 us (level)
  no operation moved by 1% of the time
where the time goes in v7:
time: 19.9 us; the launch traced here: 19.8 us
  Pallas kernels  19.1 us (96%)
  between operations  0.64 us (3%)
    pallas_call x1, Pallas kernels, on_device(): pl.pallas_call(functools.partial(kernel, layers, n), out_shape=(pltpu.VME...  18.5 us
    pallas_call x1, Pallas kernels, on_device(): pl.pallas_call(hand_over, out_shape=(jax.ShapeDtypeStruct(up_source.shape...  0.65 us

profile of v7, /device:TPU:0, one launch (start us, length us, event | category | flops | bytes accessed | tf_op | source)
XLA Modules:
  0.0 19.8 jit_solution(3859590494147035824)
XLA Ops:
  0.6 18.5 %shard_map.77 = (bf16[1,2,32,256]{3,2,1,0:T(8,128)(2,1)S(1)}, bf16[1,2,32,256]{3,2,1,0:T(8,128)(2,1)S(1)}) custom-call(bf16[1,2,32,256]{3,2,1,0:T(8,128)(2,1)} %up_hbm.1, bf16[1,2,32,256]{3,2,1,0:T(8,128)(2,1)} %down_hbm.1, s32[1,32]{1,0:T(1,128)} %bitcast.1, bf16[1,1,4,2,128,256]{5,4,3,2,1,0:T(8,128)(2,1)} %u_hbm.1, bf16[1,1,4,2,128,256]{5,4,3,2,1,0:T(8,128)(2,1)} %v_hbm.1, ...), custom_call_target="tpu_custom_call" | custom-call | tf_op jit(solution)/shard_map/pallas_call | solution.py:438
  19.1 0.6 %shard_map.78 = (bf16[1,2,32,256]{3,2,1,0:T(8,128)(2,1)}, bf16[1,2,32,256]{3,2,1,0:T(8,128)(2,1)}) custom-call(bf16[1,2,32,256]{3,2,1,0:T(8,128)(2,1)S(1)} %get-tuple-element.4.up_mem, bf16[1,2,32,256]{3,2,1,0:T(8,128)(2,1)S(1)} %get-tuple-element.5.down_mem), custom_call_target="tpu_custom_call" | custom-call | tf_op jit(solution)/shard_map/pallas_call | solution.py:470
